TPU v7x, 32 devices: a whole 2x2x4 slice. The times are simulated.
32 devices in a mesh: batch: 8 (over z, core), proto: 4 (over y, x).
Axes of the slice: x: 2, y: 2, z: 4, core: 2. Of those that a mesh axis runs over, the one named last changes fastest.
Arguments:
- student_features: bfloat16 [10, 1024, 256], P(None, 'batch'), may hold values from -8 to 8
- teacher_features: bfloat16 [2, 1024, 256], P(None, 'batch'), may hold values from -8 to 8
- student_prototypes: bfloat16 [256, 65536], P(None, 'proto'), may hold values from -0.5 to 0.5
- teacher_prototypes: bfloat16 [256, 65536], P(None, 'proto'), may hold values from -0.5 to 0.5
Outputs:
- mean_loss: float32 [], replicated
- grad_features: float32 [10, 1024, 256], P(None, ('batch', 'proto'))
- grad_prototypes: float32 [256, 65536], P('batch', 'proto')
All inputs are finite; a program needn't handle non-finite values.
Results may differ from a plain program's by a relative error of at most 0.001.
The roundings to bfloat16 on the way count: a program that leaves them out, or rounds other values in their place, can miss the bound.
Values sent between devices are 32-bit elements; how exact they have to be, the bound alone decides.
No kernel may reach another device: no remote copies, remote signals or barrier semaphores. Data moves between devices by JAX's collectives and lax.ppermute only.
A program may use at most 512 MiB of HBM per device.

v0:
```python
import math

import jax
import jax.numpy as jnp
from jax import lax
from jax.experimental import pallas as pl
from jax.experimental.pallas import tpu as pltpu
from jax.sharding import PartitionSpec as P


CLUSTER_NUMBER = 65536
SK_ITERS = 3
BATCH = "batch"
PROTO = "proto"
PAIRS = 18

STUDENT_TEMP = 0.1
TEACHER_TEMP = 0.07
NORM_EPS = 1e-06
LOG2E = math.log2(math.e)

CHUNKS = (1, 2, 2, 2, 1)
LOSS_ROWS = 8
MIB = 1 << 20
F32 = jnp.float32
BF16 = jnp.bfloat16
WHOLE = pl.BlockSpec(memory_space=pltpu.VMEM)
SCALARS = pl.BlockSpec(memory_space=pltpu.SMEM)


def vmem(shape, dtype):
    return pltpu.VMEM(shape, dtype)


def hbm(shape, dtype):
    return pltpu.HBM(shape, dtype)


def params():
    return pltpu.CompilerParams(vmem_limit_bytes=16 * MIB)


def cost(micros):
    return pl.CostEstimate(flops=int(micros * 1e9), transcendentals=0, bytes_accessed=int(micros * 1e6))


def exchange(value, axis, mask):
    size = lax.axis_size(axis)
    return lax.ppermute(value, axis, [(i, i ^ mask) for i in range(size)])


def swap(value, axis, bit):
    return exchange(value, axis, 1 << bit)


def bits_sum(value, axis, bits):
    for first in range(0, len(bits), 2):
        masks = [0]
        for bit in bits[first : first + 2]:
            masks += [mask | (1 << bit) for mask in masks]
        received = []
        for mask in masks[1:]:
            received.append(exchange(value, axis, mask))
        for part in received:
            value = value + part
    return value


def bits_of(size):
    return size.bit_length() - 1


def unit_values(values):
    def kernel(in_ref, out_ref):
        floats = in_ref[...].astype(F32)
        out_ref[...] = floats * lax.rsqrt(jnp.sum(floats * floats, axis=1, keepdims=True) + NORM_EPS)

    return pl.pallas_call(
        kernel,
        in_specs=[WHOLE],
        out_specs=WHOLE,
        out_shape=jax.ShapeDtypeStruct(values.shape, F32),
        compiler_params=params(),
        cost_estimate=cost(1),
        name="units",
    )(values)


def column_scale(floats):
    return lax.rsqrt(jnp.sum(floats * floats, axis=0, keepdims=True) + NORM_EPS)


def rows_to_lanes(partial):
    return jnp.concatenate(
        [
            jnp.sum(partial[i : i + 128].T, axis=0, keepdims=True)
            for i in range(0, partial.shape[0], 128)
        ],
        axis=1,
    )


def lanes_to_rows(values, start):
    return jnp.broadcast_to(values[:, start : start + 128], (128, 128)).T


def row_sums(place, unit, protos, width):
    rows, dim = unit.shape
    columns = protos.shape[1]
    steps = columns // width

    def kernel(place_ref, unit_ref, proto_ref, out_ref, rows_ref, sum_ref):
        step = pl.program_id(0)

        @pl.when(step == 0)
        def _():
            rows_ref[...] = unit_ref[...].astype(BF16)
            sum_ref[...] = jnp.zeros_like(sum_ref)

        for start in range(0, width, 512):
            floats = proto_ref[:, start : start + 512].astype(F32)
            proto_bf = (floats * column_scale(floats)).astype(BF16)
            cos = jnp.dot(rows_ref[...], proto_bf, preferred_element_type=F32)
            mass = jnp.exp2(cos * (LOG2E / STUDENT_TEMP))
            total = mass[:, :128]
            for lane in range(128, 512, 128):
                total = total + mass[:, lane : lane + 128]
            sum_ref[...] += total

        @pl.when(step == steps - 1)
        def _():
            out_ref[...] = jnp.zeros_like(out_ref)
            start = pl.multiple_of(place_ref[0] * rows, rows)
            out_ref[:, pl.ds(start, rows)] = rows_to_lanes(sum_ref[...])

    return pl.pallas_call(
        kernel,
        grid=(steps,),
        in_specs=[
            SCALARS,
            pl.BlockSpec((rows, dim), lambda i: (0, 0)),
            pl.BlockSpec((dim, width), lambda i: (0, i)),
        ],
        out_specs=pl.BlockSpec((1, 4 * rows), lambda i: (0, 0)),
        out_shape=jax.ShapeDtypeStruct((1, 4 * rows), F32),
        scratch_shapes=[pltpu.VMEM((rows, dim), BF16), pltpu.VMEM((rows, 128), F32)],
        compiler_params=params(),
        cost_estimate=cost(15),
        name="row_sums",
    )(place, unit, protos)


def teacher_mass(place, gathered, protos, columns, width):
    part_rows, dim = gathered[0].shape
    rows = part_rows * len(gathered)
    steps = columns // width

    def kernel(place_ref, *refs):
        parts = refs[: len(gathered)]
        proto_ref, mass_ref, sum_ref, rows_ref = refs[len(gathered) :]
        step = pl.program_id(0)

        @pl.when(step == 0)
        def _():
            for j, part in enumerate(parts):
                start = pl.multiple_of((place_ref[0] ^ j) * part_rows, part_rows)
                rows_ref[pl.ds(start, part_rows)] = part[...].astype(BF16)

        at = pl.multiple_of(step * width, width)
        part = min(512, width)
        for start in range(0, width, part):
            floats = proto_ref[:, start : start + part].astype(F32)
            proto_bf = (floats * column_scale(floats)).astype(BF16)
            cos = jnp.dot(rows_ref[...], proto_bf, preferred_element_type=F32)
            mass = jnp.exp2(cos * (LOG2E / TEACHER_TEMP))
            mass_ref[:, pl.ds(at + start, part)] = mass
            sum_ref[:, start : start + part] = jnp.sum(mass, axis=0, keepdims=True)

    return pl.pallas_call(
        kernel,
        grid_spec=pltpu.PrefetchScalarGridSpec(
            num_scalar_prefetch=1,
            grid=(steps,),
            in_specs=[pl.BlockSpec((part_rows, dim), lambda i, s: (0, 0)) for _ in gathered]
            + [pl.BlockSpec((dim, width), lambda i, s: (0, s[0] * steps + i))],
            out_specs=[WHOLE, pl.BlockSpec((1, width), lambda i, s: (0, i))],
            scratch_shapes=[pltpu.VMEM((rows, dim), BF16)],
        ),
        out_shape=[vmem((rows, columns), F32), jax.ShapeDtypeStruct((1, columns), F32)],
        compiler_params=params(),
        cost_estimate=cost(5),
        name="teacher_mass",
    )(place, *gathered, protos)


def row_pass(column_parts, mass, extra):
    rows, columns = mass.shape
    extras = [] if extra is None else [extra]
    total_rows = rows + sum(part.shape[1] for part in extras)

    def kernel(a_ref, b_ref, mass_ref, *refs):
        out_ref = refs[-1]
        scale = 1.0 / (CLUSTER_NUMBER * (a_ref[...] + b_ref[...]))

        def block(index, carry):
            start = pl.multiple_of(index * 128, 128)
            total = jnp.zeros((128, 128), F32)
            for lane in range(0, columns, 128):
                total = total + (
                    mass_ref[pl.ds(start, 128), lane : lane + 128] * scale[:, lane : lane + 128]
                )
            out_ref[:, pl.ds(start, 128)] = jnp.sum(total.T, axis=0, keepdims=True)
            return carry

        lax.fori_loop(0, rows // 128, block, 0, unroll=2)
        if extras:
            out_ref[:, rows:] = refs[0][...]

    return pl.pallas_call(
        kernel,
        in_specs=[WHOLE] * (3 + len(extras)),
        out_specs=WHOLE,
        out_shape=jax.ShapeDtypeStruct((1, total_rows), F32),
        compiler_params=params(),
        cost_estimate=cost(1.5),
        name="row_pass",
    )(*column_parts, mass, *extras)


def column_pass(row_parts, mass, sample_number):
    rows, columns = mass.shape

    def kernel(a_ref, b_ref, mass_ref, out_ref, scale_ref):
        scale = 1.0 / (sample_number * (a_ref[:, :rows] + b_ref[:, :rows]))
        for start in range(0, rows, 128):
            scale_ref[start : start + 128] = lanes_to_rows(scale, start)

        def block(index, carry):
            lane = pl.multiple_of(index * 256, 256)
            total = jnp.zeros((8, 256), F32)
            for start in range(0, rows, 128):
                scales = jnp.concatenate([scale_ref[start : start + 128]] * 2, axis=1)
                term = mass_ref[start : start + 128, pl.ds(lane, 256)] * scales
                total = total + jnp.sum(term.reshape(16, 8, 256), axis=0)
            out_ref[:, pl.ds(lane, 256)] = jnp.sum(total, axis=0, keepdims=True)
            return carry

        lax.fori_loop(0, columns // 256, block, 0, unroll=2)

    return pl.pallas_call(
        kernel,
        in_specs=[WHOLE] * 3,
        out_specs=WHOLE,
        out_shape=jax.ShapeDtypeStruct((1, columns), F32),
        scratch_shapes=[pltpu.VMEM((rows, 128), F32)],
        compiler_params=params(),
        cost_estimate=cost(1.5),
        name="column_pass",
    )(*row_parts, mass)


def gather_rows(place, own, core, far, far_core, crops, images):
    dim = own.shape[1]
    part_rows = crops * images
    pieces, _, piece_images, _ = far.shape
    rows = 4 * part_rows

    def kernel(place_ref, own_ref, core_ref, far_ref, far_core_ref, rows_ref, cols_ref, work_ref):
        def store(j, values):
            start = pl.multiple_of((place_ref[0] ^ j) * part_rows, part_rows)
            rows_ref[pl.ds(start, part_rows)] = values.astype(BF16)
            cols_ref[:, pl.ds(start, part_rows)] = values.T.astype(BF16)

        store(0, own_ref[...])
        store(1, core_ref[...])
        for j, ref in ((2, far_ref), (3, far_core_ref)):

            def move(crop, carry, ref=ref):
                for piece in range(pieces):
                    offset = (place_ref[1] ^ piece) * piece_images
                    at = pl.multiple_of(crop * images + offset, piece_images)
                    work_ref[pl.ds(at, piece_images)] = ref[piece, crop]
                return carry

            lax.fori_loop(0, crops, move, 0)
            store(j, work_ref[...])

    return pl.pallas_call(
        kernel,
        in_specs=[SCALARS] + [WHOLE] * 4,
        out_specs=[WHOLE] * 2,
        out_shape=[vmem((rows, dim), BF16), vmem((dim, rows), BF16)],
        scratch_shapes=[pltpu.VMEM((part_rows, dim), F32)],
        compiler_params=params(),
        cost_estimate=cost(3),
        name="gather_rows",
    )(place, own, core, far, far_core)


def row_offsets(parts, skip, crops, images, factor):
    rows = parts[0].shape[1] - skip

    def kernel(a_ref, b_ref, out_ref, norm_ref, sums_ref):
        sums_ref[...] = a_ref[:, skip:] + b_ref[:, skip:]

        def block(index, total):
            start = pl.multiple_of(index * 128, 128)
            pair_count = jnp.where((start // images) % crops < 2, F32(1.0), F32(2.0))
            sums = sums_ref[:, pl.ds(start, 128)]
            out_ref[pl.ds(start, 128)] = lanes_to_rows(jnp.log2((pair_count * factor) / sums), 0)
            return total + pair_count * jnp.log(sums)

        total = lax.fori_loop(0, rows // 128, block, jnp.zeros((1, 128), F32), unroll=10)
        norm_ref[...] = jnp.sum(total, axis=1, keepdims=True) + jnp.zeros((1, 128), F32)

    return pl.pallas_call(
        kernel,
        in_specs=[WHOLE] * 2,
        out_specs=[WHOLE] * 2,
        out_shape=[vmem((rows, 128), F32), jax.ShapeDtypeStruct((1, 128), F32)],
        scratch_shapes=[pltpu.VMEM((1, rows), F32)],
        compiler_params=params(),
        cost_estimate=cost(1),
        name="row_offsets",
    )(*parts)


def gradients(place, steps, first, last, protos, mass, column_sums, row_sum, rows, cols, offsets, norm_sum, carried, geometry):
    crops, images, pieces, blocks, factor, order = geometry
    dim = protos.shape[0]
    half = dim // 2
    out_rows = half + (LOSS_ROWS if last else 0)
    row_count = rows.shape[0]
    teacher_rows, columns = mass.shape
    groups = teacher_rows // (2 * images)
    part_rows = crops * images
    piece_images = images // pieces
    total_steps = sum(CHUNKS)
    width = columns // total_steps
    block_rows = dim // blocks

    def kernel(place_ref, *refs):
        refs = list(refs)
        proto_ref, mass_ref, csum_ref, rsum_ref, rows_ref, cols_ref, offs_ref = refs[:7]
        refs = refs[7:]
        if last:
            norm_ref = refs.pop(0)
        if not first:
            feat_in, targ_in = refs[:2]
            refs = refs[2:]
        send_ref, keep_ref = refs[:2]
        refs = refs[2:]
        if last:
            wing_refs = refs[:4]
            refs = refs[4:]
            sem_ref = refs.pop()
            feat_ref, targ_ref = feat_in, targ_in
        else:
            feat_ref, targ_ref = refs[:2]
            refs = refs[2:]
        grad_ref, tbf_ref, rscale_ref, weight_ref, *cos_refs = refs
        step = pl.program_id(0)

        @pl.when(step == 0)
        def _():
            scale = factor / rsum_ref[...]
            for start in range(0, teacher_rows, 128):
                rscale_ref[start : start + 128] = lanes_to_rows(scale, start)
            if first:

                def clear(crop, carry):
                    feat_ref[:, pl.ds(crop, 1)] = jnp.zeros((groups, 1, images, dim), F32)
                    return carry

                lax.fori_loop(0, crops, clear, 0)
                targ_ref[...] = jnp.zeros_like(targ_ref)

        at = pl.multiple_of((place_ref[3] + step) * width, width)
        floats = proto_ref[...].astype(F32)
        inverse = column_scale(floats)
        unit = floats * inverse
        proto_bf = unit.astype(BF16)
        proto_t = unit.T.astype(BF16)
        cscale = 1.0 / (CLUSTER_NUMBER * csum_ref[:, pl.ds(at, width)])

        for group in range(groups):
            base = group * part_rows
            tbase = group * 2 * images
            cos_ref = cos_refs[group % 2]
            cos_ref[...] = jnp.dot(rows_ref[base : base + part_rows], proto_bf, preferred_element_type=F32)
            for lane in range(0, width, 128):
                lanes = slice(lane, lane + 128)
                for image in range(0, images, 64):
                    pair = []
                    for wide in range(2):
                        start = tbase + wide * images + image
                        target = (
                            mass_ref[start : start + 64, pl.ds(at + lane, 128)]
                            * rscale_ref[start : start + 64]
                            * cscale[:, lanes]
                        )
                        tbf_ref[start : start + 64, lanes] = target.astype(BF16)
                        pair.append(target)
                    both = pair[0] + pair[1]
                    for crop in range(crops):
                        start = crop * images + image
                        power = cos_ref[start : start + 64, lanes] * (LOG2E / STUDENT_TEMP)
                        prob = jnp.exp2(power + offs_ref[base + start : base + start + 64])
                        target = pair[1] if crop == 0 else pair[0] if crop == 1 else both
                        grad_ref[base + start : base + start + 64, lanes] = (prob - target).astype(BF16)
            product = jnp.dot(grad_ref[base : base + part_rows], proto_t, preferred_element_type=F32)
            feat_ref[group] += product.reshape(crops, images, dim)
        copies = []
        if last:
            for j in range(4):
                dest = wing_refs[(j >> 1) + (0 if j & 1 else 2)]
                for piece in range(pieces):
                    start = pl.multiple_of((place_ref[2] ^ piece) * piece_images, piece_images)
                    copies.append(
                        pltpu.make_async_copy(
                            feat_ref.at[place_ref[0] ^ j, :, pl.ds(start, piece_images)],
                            dest.at[piece],
                            sem_ref.at[len(copies)],
                        )
                    )
                    copies[-1].start()
        targ_ref[...] += jnp.dot(tbf_ref[...], proto_t, preferred_element_type=F32)
        weight_ref[...] = jnp.zeros_like(weight_ref)

        def part_of_rows(index, carry):
            part = pl.ds(pl.multiple_of(index * (row_count // 2), row_count // 2), row_count // 2)
            weight_ref[...] += jnp.dot(cols_ref[:, part], grad_ref[part], preferred_element_type=F32)
            return carry

        lax.fori_loop(0, 2, part_of_rows, 0)
        weight = weight_ref[...]
        curvature = jnp.sum(proto_bf.astype(F32) * weight, axis=0, keepdims=True)
        weight_ref[...] = inverse * (weight - unit * curvature)
        for position, j in enumerate(order):
            start = pl.multiple_of((place_ref[1] ^ j) * block_rows, block_rows)
            dest, index = (keep_ref, position) if position < blocks // 2 else (send_ref, position - blocks // 2)
            dest[index * block_rows : (index + 1) * block_rows] = weight_ref[pl.ds(start, block_rows)]

        if last:
            total = jnp.zeros((images, dim), F32)
            for group in range(groups):
                base = group * part_rows
                tbase = group * 2 * images
                crop_rows = [
                    rows_ref[base + c * images : base + (c + 1) * images].astype(F32) for c in range(crops)
                ]
                shared = crop_rows[2]
                for c in range(3, crops):
                    shared = shared + crop_rows[c]
                total = total + targ_ref[tbase : tbase + images] * (crop_rows[1] + shared)
                total = total + targ_ref[tbase + images : tbase + 2 * images] * (crop_rows[0] + shared)
            product = jnp.sum(jnp.sum(total, axis=0, keepdims=True), axis=1, keepdims=True)
            loss = norm_ref[:, :1] * (1.0 / (4 * pieces)) - product * (1.0 / (factor * STUDENT_TEMP))
            keep_ref[half:] = loss + jnp.zeros((LOSS_ROWS, width), F32)
            send_ref[half:] = loss + jnp.zeros((LOSS_ROWS, width), F32)
            for copy in copies:
                copy.wait()

    out_shape = [hbm((out_rows, steps * width), F32)] * 2
    out_specs = [pl.BlockSpec((out_rows, width), lambda i, s: (0, i))] * 2
    operands = [protos, mass, column_sums, row_sum, rows, cols, offsets]
    in_specs = [
        pl.BlockSpec((dim, width), lambda i, s: (0, s[0] * total_steps + s[3] + i)),
    ] + [WHOLE] * 6
    aliases = {}
    scratch = []
    if last:
        operands.append(norm_sum)
        in_specs.append(WHOLE)
    if not first:
        operands += list(carried)
        in_specs += [WHOLE] * 2
    if last:
        shape = (pieces, crops, piece_images, dim)
        out_shape = out_shape + [hbm(shape, F32)] * 4
        out_specs = out_specs + [pl.BlockSpec(memory_space=pl.ANY)] * 4
    else:
        out_shape = out_shape + [vmem((groups, crops, images, dim), F32), vmem((teacher_rows, dim), F32)]
        out_specs = out_specs + [WHOLE] * 2
        if not first:
            aliases = {8: 2, 9: 3}
    scratch += [
        pltpu.VMEM((row_count, width), BF16),
        pltpu.VMEM((teacher_rows, width), BF16),
        pltpu.VMEM((teacher_rows, 128), F32),
        pltpu.VMEM((dim, width), F32),
        pltpu.VMEM((part_rows, width), F32),
        pltpu.VMEM((part_rows, width), F32),
    ]
    if last:
        assert steps == 1 and not first
        scratch.append(pltpu.SemaphoreType.DMA((4 * pieces,)))
    return pl.pallas_call(
        kernel,
        grid_spec=pltpu.PrefetchScalarGridSpec(
            num_scalar_prefetch=1, grid=(steps,), in_specs=in_specs, out_specs=out_specs, scratch_shapes=scratch
        ),
        out_shape=out_shape,
        input_output_aliases=aliases,
        compiler_params=params(),
        cost_estimate=cost(10),
        name="gradients",
    )(place, *operands)


def assemble(place, pieces, first, base):
    rows = pieces[0][0].shape[0]
    count = 4 * len(pieces)
    quarter = sum(CHUNKS)
    unit = pieces[0][0].shape[1] // CHUNKS[first]
    columns = 4 * quarter * unit
    flat = [piece for chunk in pieces for piece in chunk]

    def kernel(place_ref, *refs):
        out_ref, sem_ref = refs[-2:]
        copies = []
        for chunk in range(len(pieces)):
            width = CHUNKS[first + chunk] * unit
            offset = sum(CHUNKS[: first + chunk]) * unit
            for j in range(4):
                at = pl.multiple_of((place_ref[0] ^ j) * (quarter * unit) + offset, 128)
                index = 4 * chunk + j
                copies.append(
                    pltpu.make_async_copy(refs[index], out_ref.at[:, pl.ds(at, width)], sem_ref.at[index])
                )
                copies[-1].start()
        for copy in copies:
            copy.wait()

    anywhere = pl.BlockSpec(memory_space=pl.ANY)
    operands = flat if base is None else flat + [base]
    return pl.pallas_call(
        kernel,
        in_specs=[SCALARS] + [anywhere] * len(operands),
        out_specs=anywhere,
        out_shape=jax.ShapeDtypeStruct((rows, columns), F32),
        scratch_shapes=[pltpu.SemaphoreType.DMA((count,))],
        input_output_aliases={} if base is None else {1 + count: 0},
        compiler_params=params(),
        cost_estimate=cost(1.5),
        name="assemble",
    )(place, *operands)


def finish(near, received, unit, raw):
    shape = near.shape
    rows = [value.reshape(-1, shape[-1]) for value in (near, received, unit, raw)]

    def kernel(near_ref, received_ref, unit_ref, raw_ref, out_ref):
        cotangent = near_ref[...] + received_ref[...]
        unit = unit_ref[...]
        floats = raw_ref[...].astype(F32)
        scale = lax.rsqrt(jnp.sum(floats * floats, axis=1, keepdims=True) + NORM_EPS)
        out_ref[...] = scale * (cotangent - unit * jnp.sum(unit * cotangent, axis=1, keepdims=True))

    return pl.pallas_call(
        kernel,
        in_specs=[WHOLE] * 4,
        out_specs=WHOLE,
        out_shape=jax.ShapeDtypeStruct(rows[0].shape, F32),
        compiler_params=params(),
        cost_estimate=cost(1),
        name="finish",
    )(*rows).reshape(shape)


def step_on_device(student_features, teacher_features, student_prototypes, teacher_prototypes):
    student_prototypes = pltpu.with_memory_space_constraint(student_prototypes, pltpu.HBM)
    teacher_prototypes = pltpu.with_memory_space_constraint(teacher_prototypes, pltpu.HBM)
    crops, images, dim = student_features.shape
    proto_local = student_prototypes.shape[1]
    batch_devices = lax.axis_size(BATCH)
    proto_devices = lax.axis_size(PROTO)
    batch_bits = bits_of(batch_devices)
    proto_bits = bits_of(proto_devices)
    images_all = images * batch_devices
    sample_number = teacher_features.shape[0] * images_all
    factor = 1.0 / (images_all * PAIRS * STUDENT_TEMP)
    batch_index = lax.axis_index(BATCH)
    proto_index = lax.axis_index(PROTO)
    core, top = 0, batch_bits - 1
    middle = list(range(1, top))
    place = ((batch_index >> top) & 1) * 2 + (batch_index & 1)
    own_images = images // proto_devices
    columns = proto_local // 4
    places = jnp.stack([place, batch_index, proto_index]).astype(jnp.int32)
    chunk_places = [
        jnp.stack([place, batch_index, proto_index, jnp.int32(sum(CHUNKS[:chunk]))]).astype(jnp.int32)
        for chunk in range(len(CHUNKS))
    ]
    row_places = jnp.stack([place, proto_index]).astype(jnp.int32)

    teacher_own = unit_values(teacher_features.reshape(-1, dim))
    teacher_core = swap(teacher_own, BATCH, core)
    teacher_far = swap(teacher_own, BATCH, top)
    teacher_far_core = swap(teacher_far, BATCH, core)

    own_rows = unit_values(student_features.reshape(-1, dim))
    all_sums = row_sums(places, own_rows, student_prototypes, min(1024, proto_local))

    mass, column_sum = teacher_mass(
        places,
        [teacher_own, teacher_core, teacher_far, teacher_far_core],
        teacher_prototypes,
        columns,
        min(1024, columns),
    )

    own_start = proto_index * own_images
    unit_own = lax.dynamic_slice_in_dim(own_rows.reshape(crops, images, dim), own_start, own_images, 1)
    raw_own = lax.dynamic_slice_in_dim(student_features, own_start, own_images, 1)
    far = swap(unit_own, BATCH, top)[None]
    for bit in range(proto_bits):
        received = swap(far, PROTO, bit)
        far = jnp.concatenate([far, received], axis=0)
    core_rows = swap(own_rows, BATCH, core)
    far_core = swap(far, BATCH, core)
    rows, cols = gather_rows(row_places, own_rows, core_rows, far, far_core, crops, images)

    row_parts = None
    for sweep_index in range(SK_ITERS):
        if sweep_index:
            column_sum = column_pass(row_parts, mass, sample_number)
        for bit in middle[:-1]:
            column_sum = column_sum + swap(column_sum, BATCH, bit)
        column_parts = (column_sum, swap(column_sum, BATCH, middle[-1]))
        row_sum = row_pass(column_parts, mass, None if sweep_index else all_sums)
        row_sum = bits_sum(row_sum, PROTO, range(proto_bits))
        received = swap(row_sum, BATCH, top)
        row_sum = row_sum + received
        row_parts = (row_sum, swap(row_sum, BATCH, core))
        if sweep_index == 0:
            offsets, norm_sum = row_offsets(row_parts, mass.shape[0], crops, images, factor)

    row_total = row_parts[0] + row_parts[1]
    column_total = column_parts[0] + column_parts[1]
    order = [0]
    for bit in [core, top] + middle[::-1]:
        order = order + [j | (1 << bit) for j in order]
    geometry = (crops, images, proto_devices, batch_devices, factor, order)
    carried = None
    pieces = []
    for chunk, steps in enumerate(CHUNKS):
        outs = gradients(
            chunk_places[chunk], steps, chunk == 0, chunk == len(CHUNKS) - 1, student_prototypes, mass,
            column_total, row_total, rows, cols, offsets, norm_sum, carried, geometry,
        )
        send, keep = outs[:2]
        carried = outs[2:]
        loss_rows = LOSS_ROWS if chunk == len(CHUNKS) - 1 else 0
        for bit in middle[:-1]:
            keep = keep + swap(send, BATCH, bit)
            end = keep.shape[0] - loss_rows
            send = keep[end // 2 :]
            keep = jnp.concatenate([keep[: end // 2], keep[end:]], axis=0)
        half = (keep.shape[0] - loss_rows) // 2
        quarter = half // 2
        received = swap(send, BATCH, middle[-1])
        far_send = keep[half:] + received[half:]
        near_own = keep[:quarter] + received[:quarter]
        near_core = keep[quarter:half] + received[quarter:half]
        far_half = swap(far_send, BATCH, top)
        near_core = swap(near_core, BATCH, core)
        far_core = far_half[quarter:half]
        if loss_rows:
            loss = far_send[half:] + far_half[half:]
            far_core = jnp.concatenate([far_core, loss], axis=0)
        far_core = swap(far_core, BATCH, core)
        if loss_rows:
            loss = (loss + far_core[quarter:])[:1, :128]
        pieces.append([near_own, near_core, far_half[:quarter], far_core[:quarter]])
    early = len(CHUNKS) - 2
    grad_prototypes = assemble(places, pieces[:early], 0, None)
    grad_prototypes = assemble(places, pieces[early:], early, grad_prototypes)

    far_wings, near_wings = carried[:2], carried[2:]
    received = [swap(far_wings[1], BATCH, core)]
    received = [swap(far_wings[0], BATCH, core)] + received
    totals = []
    for wing in range(2):
        part = (near_wings[wing] + received[wing]).reshape((2,) * proto_bits + (crops, own_images, dim))
        axes = list(range(proto_bits))
        axes = axes[wing % proto_bits :] + axes[: wing % proto_bits]
        for axis in axes:
            bit = proto_bits - 1 - axis
            near = lax.slice_in_dim(part, 0, 1, axis=axis)
            away = lax.slice_in_dim(part, 1, 2, axis=axis)
            part = near + swap(away, PROTO, bit)
        totals.append(part.reshape(crops, own_images, dim))
    received = swap(totals[1], BATCH, top)
    grad_features = finish(totals[0], received, unit_own, raw_own)

    loss = bits_sum(loss, PROTO, range(proto_bits))
    mean_loss = loss[0, 0] / (images_all * PAIRS)
    return (mean_loss, grad_features, grad_prototypes)


def solution(mesh):
    placed = (P(None, BATCH, None), P(None, BATCH, None), P(None, PROTO), P(None, PROTO))
    return jax.shard_map(
        step_on_device,
        mesh=mesh,
        in_specs=placed,
        out_specs=(P(), P(None, (BATCH, PROTO), None), P(BATCH, PROTO)),
        check_vma=False,
    )
```

profile of v0, /device:TPU:0, one launch (start us, length us, event | category | flops | bytes accessed | tf_op | source)
XLA Modules:
  0.0 309.7 jit_solution(1955666820819324853)
XLA Ops:
  1.7 4.1 %collective-permute-start.1 = (f32[256,256]{1,0:T(8,128)S(1)}, f32[256,256]{1,0:T(8,128)S(1)}, u32[]{:S(2)}, u32[]{:S(2)}) collective-permute-start(f32[256,256]{1,0:T(8,128)S(1)} %units.2.refs_0_), channel_id=1, source_target_pairs={{0,16},{4,20},{8,24},{12,28},{16,0},{20,4},{24,8},{28,12},{1,17},{... | collective-permute-start | bytes 786440 | tf_op jit(solution)/shard_map/ppermute | solution.py:49
  6.1 1.0 collective-permute-start.22
  7.2 18.4 %collective-permute-done.1.refs_2_ = f32[256,256]{1,0:T(8,128)S(1)} collective-permute-done((f32[256,256]{1,0:T(8,128)S(1)}, f32[256,256]{1,0:T(8,128)S(1)}, u32[]{:S(2)}, u32[]{:S(2)}) %collective-permute-start.1) | collective-permute-done | bytes 262176 | tf_op jit(solution)/shard_map/ppermute | solution.py:49
  26.4 5.5 %collective-permute-done.22 = f32[10,32,256]{2,1,0:T(8,128)} collective-permute-done((f32[10,32,256]{2,1,0:T(8,128)S(1)}, f32[10,32,256]{2,1,0:T(8,128)}, u32[]{:S(2)}, u32[]{:S(2)}) %collective-permute-start.22) | collective-permute-done | bytes 327712 | tf_op jit(solution)/shard_map/ppermute | solution.py:49
  31.9 1.5 collective-permute-start.23
  34.1 0.9 copy-done.2
  37.0 5.3 %teacher_mass.1 = (f32[1024,4096]{1,0:T(8,128)S(1)}, f32[1,4096]{1,0:T(1,128)S(1)}) custom-call(s32[3]{0:T(128)S(1)} %pad_add_fusion.2.place_ref, f32[256,256]{1,0:T(8,128)S(1)} %copy-done.2, f32[256,256]{1,0:T(8,128)S(1)} %copy-done.6, f32[256,256]{1,0:T(8,128)S(1)} %copy-done.4, f32[256,256]{1,0:T(8,128)} %collective-permute-done.2.refs_3_, ...), custom_call_target="tpu_custom_call" | custom-call | flops 5000000000 | bytes 5000000 | tf_op jit(solution)/shard_map/teacher_mass/pallas_call | solution.py:179
  42.9 17.3 %row_sums.1.refs_0_ = f32[1,5120]{1,0:T(1,128)S(1)} custom-call(s32[3]{0:T(128)S(1)} %pad_add_fusion.2.place_ref, f32[1280,256]{1,0:T(8,128)S(1)} %units.3.unit_ref.own_ref, bf16[256,16384]{1,0:T(8,128)(2,1)} %refs_0_.9), custom_call_target="tpu_custom_call" | custom-call | flops 15000000512 | bytes 15000000 | tf_op jit(solution)/shard_map/row_sums/pallas_call | solution.py:136
  60.2 1.5 row_pass.3
  62.4 1.5 collective-permute-start.5
  63.9 1.4 collective-permute-start.6
  65.3 1.0 pad_maximum_fusion.1
  66.4 1.6 collective-permute-start.24
  68.8 3.5 %collective-permute-start.7 = (f32[1,6144]{1,0:T(1,128)S(1)}, f32[1,6144]{1,0:T(1,128)S(1)}, u32[]{:S(2)}, u32[]{:S(2)}) collective-permute-start(f32[1,6144]{1,0:T(1,128)S(1)} %add_add_fusion), channel_id=1, source_target_pairs={{0,16},{4,20},{8,24},{12,28},{16,0},{20,4},{24,8},{28,12},{1,17},{... | collective-permute-start | bytes 73736 | tf_op jit(solution)/shard_map/ppermute | solution.py:49
  72.3 1.8 collective-permute-done.7
  75.4 2.1 column_pass.2.a_ref
  77.5 1.0 collective-permute-start.9
  78.5 3.5 %collective-permute-done.24 = f32[2,10,32,256]{3,2,1,0:T(8,128)S(1)} collective-permute-done((f32[2,10,32,256]{3,2,1,0:T(8,128)S(1)}, f32[2,10,32,256]{3,2,1,0:T(8,128)S(1)}, u32[]{:S(2)}, u32[]{:S(2)}) %collective-permute-start.24) | collective-permute-done | bytes 655392 | tf_op jit(solution)/shard_map/ppermute | solution.py:49
  82.0 1.1 pad_maximum_fusion.far_ref
  83.1 1.5 row_pass.4
  85.2 1.5 collective-permute-start.11
  86.8 1.4 collective-permute-start.12
  88.9 2.4 collective-permute-done.12
  91.3 3.6 %collective-permute-start.13 = (f32[1,1024]{1,0:T(1,128)S(1)}, f32[1,1024]{1,0:T(1,128)S(1)}, u32[]{:S(2)}, u32[]{:S(2)}) collective-permute-start(f32[1,1024]{1,0:T(1,128)S(1)} %add_add_fusion.2), channel_id=1, source_target_pairs={{0,16},{4,20},{8,24},{12,28},{16,0},{20,4},{24,8},{28,12},{1,17},{... | collective-permute-start | bytes 12296 | tf_op jit(solution)/shard_map/ppermute | solution.py:49
  94.8 1.6 collective-permute-done.13
  96.4 1.2 collective-permute-done.14.b_ref
  97.6 2.1 column_pass.3.a_ref
  100.1 3.4 %collective-permute-done.15.b_ref = f32[1,4096]{1,0:T(1,128)S(1)} collective-permute-done((f32[1,4096]{1,0:T(1,128)S(1)}, f32[1,4096]{1,0:T(1,128)S(1)}, u32[]{:S(2)}, u32[]{:S(2)}) %collective-permute-start.15) | collective-permute-done | bytes 16416 | tf_op jit(solution)/shard_map/ppermute | solution.py:49
  103.5 1.5 row_pass.5
  105.0 1.3 collective-permute-start.16
  107.1 1.5 collective-permute-start.18
  108.7 1.2 collective-permute-done.17
  109.9 1.7 collective-permute-done.18
  111.6 3.0 collective-permute-start.19
  114.6 1.5 collective-permute-done.19
  116.2 1.1 row_offsets.1
  117.4 1.8 gather_rows.1
  119.2 8.6 %gradients.5 = (f32[128,512]{1,0:T(8,128)}, f32[128,512]{1,0:T(8,128)}, f32[4,10,128,256]{3,2,1,0:T(8,128)S(1)}, f32[1024,256]{1,0:T(8,128)S(1)}) custom-call(s32[4]{0:T(128)S(1)} %get-tuple-element.59.place_ref, bf16[256,16384]{1,0:T(8,128)(2,1)} %refs_0_.9, f32[1024,4096]{1,0:T(8,128)S(1)} %get-tuple-element.31.mass_ref.refs_1_, ...), custom_call_target="tpu_custom_call" | custom-call | flops 10000000000 | bytes 10000000 | tf_op jit(solution)/shard_map/gradients/pallas_call | solution.py:498
  128.0 14.0 %gradients.6 = (f32[128,1024]{1,0:T(8,128)}, f32[128,1024]{1,0:T(8,128)}, f32[4,10,128,256]{3,2,1,0:T(8,128)S(1)}, f32[1024,256]{1,0:T(8,128)S(1)}) custom-call(s32[4]{0:T(128)S(1)} %get-tuple-element.81.place_ref, bf16[256,16384]{1,0:T(8,128)(2,1)} %refs_0_.9, ...), custom_call_target="tpu_custom_call", output_to_operand_aliasing={{2}: (8, {}), {3}: (9, {})} | custom-call | flops 10000000000 | bytes 10000000 | tf_op jit(solution)/shard_map/gradients/pallas_call | solution.py:498
  142.0 13.8 %gradients.7 = (f32[128,1024]{1,0:T(8,128)}, f32[128,1024]{1,0:T(8,128)}, f32[4,10,128,256]{3,2,1,0:T(8,128)S(1)}, f32[1024,256]{1,0:T(8,128)S(1)}) custom-call(s32[4]{0:T(128)S(1)} %get-tuple-element.82.place_ref, bf16[256,16384]{1,0:T(8,128)(2,1)} %refs_0_.9, ...), custom_call_target="tpu_custom_call", output_to_operand_aliasing={{2}: (8, {}), {3}: (9, {})} | custom-call | flops 10000000000 | bytes 10000000 | tf_op jit(solution)/shard_map/gradients/pallas_call | solution.py:498
  155.8 14.0 %gradients.8 = (f32[128,1024]{1,0:T(8,128)}, f32[128,1024]{1,0:T(8,128)}, f32[4,10,128,256]{3,2,1,0:T(8,128)S(1)}, f32[1024,256]{1,0:T(8,128)S(1)}) custom-call(s32[4]{0:T(128)S(1)} %get-tuple-element.83.place_ref, bf16[256,16384]{1,0:T(8,128)(2,1)} %refs_0_.9, ...), custom_call_target="tpu_custom_call", output_to_operand_aliasing={{2}: (8, {}), {3}: (9, {})} | custom-call | flops 10000000000 | bytes 10000000 | tf_op jit(solution)/shard_map/gradients/pallas_call | solution.py:498
  169.8 9.0 %gradients.9 = (f32[136,512]{1,0:T(8,128)}, f32[136,512]{1,0:T(8,128)}, f32[4,10,32,256]{3,2,1,0:T(8,128)}, f32[4,10,32,256]{3,2,1,0:T(8,128)}, f32[4,10,32,256]{3,2,1,0:T(8,128)}, /*index=5*/f32[4,10,32,256]{3,2,1,0:T(8,128)}) custom-call(s32[4]{0:T(128)S(1)} %get-tuple-element.84.place_ref, bf16[256,16384]{1,0:T(8,128)(2,1)} %refs_0_.9, ...), custom_call_target="tpu_custom_call" | custom-call | flops 10000000000 | bytes 10000000 | tf_op jit(solution)/shard_map/gradients/pallas_call | solution.py:498
  178.8 1.8 collective-permute-start.26
  181.0 1.7 collective-permute-start.48
  182.8 3.0 collective-permute-start.46
  185.8 5.7 %collective-permute-done.26 = f32[136,512]{1,0:T(8,128)S(1)} collective-permute-done((f32[136,512]{1,0:T(8,128)}, f32[136,512]{1,0:T(8,128)S(1)}, u32[]{:S(2)}, u32[]{:S(2)}) %collective-permute-start.26) | collective-permute-done | bytes 278560 | tf_op jit(solution)/shard_map/ppermute | solution.py:49
  192.4 2.3 collective-permute-start.27
  194.7 20.8 %collective-permute-done.27 = f32[72,512]{1,0:T(8,128)S(1)} collective-permute-done((f32[72,512]{1,0:T(8,128)S(1)}, f32[72,512]{1,0:T(8,128)S(1)}, u32[]{:S(2)}, u32[]{:S(2)}) %collective-permute-start.27) | collective-permute-done | bytes 147488 | tf_op jit(solution)/shard_map/ppermute | solution.py:49
  217.5 1.5 collective-permute-start.30
  219.0 1.4 collective-permute-start.31
  220.5 3.7 %collective-permute-start.39 = (f32[128,1024]{1,0:T(8,128)S(1)}, f32[128,1024]{1,0:T(8,128)S(1)}, u32[]{:S(2)}, u32[]{:S(2)}) collective-permute-start(f32[128,1024]{1,0:T(8,128)S(1)} %copy-done.15), channel_id=1, source_target_pairs={{0,8},{4,12},{8,0},{12,4},{16,24},{20,28},{24,16},{28,20},{1,9},{5... | collective-permute-start | bytes 1572872 | tf_op jit(solution)/shard_map/ppermute | solution.py:49
  225.6 10.1 %collective-permute-done.39 = f32[128,1024]{1,0:T(8,128)S(1)} collective-permute-done((f32[128,1024]{1,0:T(8,128)S(1)}, f32[128,1024]{1,0:T(8,128)S(1)}, u32[]{:S(2)}, u32[]{:S(2)}) %collective-permute-start.39) | collective-permute-done | bytes 524320 | tf_op jit(solution)/shard_map/ppermute | solution.py:49
  235.7 1.4 collective-permute-start.54
  237.2 12.0 %collective-permute-done.54 = f32[64,1024]{1,0:T(8,128)S(1)} collective-permute-done((f32[64,1024]{1,0:T(8,128)S(1)}, f32[64,1024]{1,0:T(8,128)S(1)}, u32[]{:S(2)}, u32[]{:S(2)}) %collective-permute-start.54) | collective-permute-done | bytes 262176 | tf_op jit(solution)/shard_map/ppermute | solution.py:49
  249.3 3.0 collective-permute-start.41
  254.1 13.2 %collective-permute-done.50 = f32[64,1024]{1,0:T(8,128)S(1)} collective-permute-done((f32[64,1024]{1,0:T(8,128)S(1)}, f32[64,1024]{1,0:T(8,128)S(1)}, u32[]{:S(2)}, u32[]{:S(2)}) %collective-permute-start.50) | collective-permute-done | bytes 262176 | tf_op jit(solution)/shard_map/ppermute | solution.py:49
  267.3 1.2 collective-permute-start.33
  268.6 4.3 %collective-permute-done.41 = f32[64,1024]{1,0:T(8,128)S(1)} collective-permute-done((f32[64,1024]{1,0:T(8,128)S(1)}, f32[64,1024]{1,0:T(8,128)S(1)}, u32[]{:S(2)}, u32[]{:S(2)}) %collective-permute-start.41) | collective-permute-done | bytes 262176 | tf_op jit(solution)/shard_map/ppermute | solution.py:49
  275.0 1.2 collective-permute-start.37
  276.2 1.7 assemble.2.refs_8_
  277.9 7.0 %collective-permute-done.33 = f32[1,2,10,32,256]{4,3,2,1,0:T(8,128)S(1)} collective-permute-done((f32[1,2,10,32,256]{4,3,2,1,0:T(8,128)S(1)}, f32[1,2,10,32,256]{4,3,2,1,0:T(8,128)S(1)}, u32[]{:S(2)}, u32[]{:S(2)}) %collective-permute-start.33) | collective-permute-done | bytes 655392 | tf_op jit(solution)/shard_map/ppermute | solution.py:49
  285.7 5.2 %collective-permute-done.37 = f32[1,1,10,32,256]{4,3,2,1,0:T(8,128)S(1)} collective-permute-done((f32[1,1,10,32,256]{4,3,2,1,0:T(8,128)S(1)}, f32[1,1,10,32,256]{4,3,2,1,0:T(8,128)S(1)}, u32[]{:S(2)}, u32[]{:S(2)}) %collective-permute-start.37) | collective-permute-done | bytes 327712 | tf_op jit(solution)/shard_map/ppermute | solution.py:49
  291.1 1.5 assemble.3
  292.8 14.8 %collective-permute-done.38 = f32[10,32,256]{2,1,0:T(8,128)S(1)} collective-permute-done((f32[10,32,256]{2,1,0:T(8,128)S(1)}, f32[10,32,256]{2,1,0:T(8,128)S(1)}, u32[]{:S(2)}, u32[]{:S(2)}) %collective-permute-start.38) | collective-permute-done | bytes 327712 | tf_op jit(solution)/shard_map/ppermute | solution.py:49
  (150 shorter events, 21.9 us)
Async XLA Ops:
  1.7 23.9 %collective-permute-start.1 = (f32[256,256]{1,0:T(8,128)S(1)}, f32[256,256]{1,0:T(8,128)S(1)}, u32[]{:S(2)}, u32[]{:S(2)}) collective-permute-start(f32[256,256]{1,0:T(8,128)S(1)} %units.2.refs_0_), channel_id=1, source_target_pairs={{0,16},{4,20},{8,24},{12,28},{16,0},{20,4},{24,8},{28,12},{1,17},{... | collective-permute-start | bytes 786440 | tf_op jit(solution)/shard_map/ppermute | solution.py:49
  6.1 25.8 %collective-permute-start.22 = (f32[10,32,256]{2,1,0:T(8,128)S(1)}, f32[10,32,256]{2,1,0:T(8,128)}, u32[]{:S(2)}, u32[]{:S(2)}) collective-permute-start(f32[10,32,256]{2,1,0:T(8,128)S(1)} %constant_dynamic-slice_fusion.1), channel_id=1, source_target_pairs={{0,16},{4,20},{8,24},{12,28},{16,0},{20,4},{24,8},{28,12},{1,17},{... | collective-permute-start | bytes 983048 | tf_op jit(solution)/shard_map/ppermute | solution.py:49
  7.2 26.3 %collective-permute-start = (f32[256,256]{1,0:T(8,128)S(1)}, f32[256,256]{1,0:T(8,128)S(1)}, u32[]{:S(2)}, u32[]{:S(2)}) collective-permute-start(f32[256,256]{1,0:T(8,128)S(1)} %units.2.refs_0_), channel_id=1, source_target_pairs={{0,4},{4,0},{8,12},{12,8},{16,20},{20,16},{24,28},{28,24},{1,5},{5... | collective-permute-start | bytes 786440 | tf_op jit(solution)/shard_map/ppermute | solution.py:49
  25.6 8.5 %collective-permute-start.2 = (f32[256,256]{1,0:T(8,128)S(1)}, f32[256,256]{1,0:T(8,128)}, u32[]{:S(2)}, u32[]{:S(2)}) collective-permute-start(f32[256,256]{1,0:T(8,128)S(1)} %collective-permute-done.1.refs_2_), channel_id=1, source_target_pairs={{0,4},{4,0},{8,12},{12,8},{16,20},{20,16},{24,28},{28,24},{1,5},{5... | collective-permute-start | bytes 786440 | tf_op jit(solution)/shard_map/ppermute | solution.py:49
  31.9 33.5 %collective-permute-start.23 = (f32[1,10,32,256]{3,2,1,0:T(8,128)}, f32[1,10,32,256]{3,2,1,0:T(8,128)S(1)}, u32[]{:S(2)}, u32[]{:S(2)}) collective-permute-start(f32[1,10,32,256]{3,2,1,0:T(8,128)} %bitcast.6), channel_id=1, source_target_pairs={{0,1},{1,0},{2,3},{3,2},{4,5},{5,4},{6,7},{7,6},{8,9},{9,8},{10,11... | collective-permute-start | bytes 983048 | tf_op jit(solution)/shard_map/ppermute | solution.py:49
  42.3 18.0 %collective-permute-start.3 = (f32[1,4096]{1,0:T(1,128)S(1)}, f32[1,4096]{1,0:T(1,128)S(1)}, u32[]{:S(2)}, u32[]{:S(2)}) collective-permute-start(f32[1,4096]{1,0:T(1,128)S(1)} %get-tuple-element.32.a_ref), channel_id=1, source_target_pairs={{0,8},{4,12},{8,0},{12,4},{16,24},{20,28},{24,16},{28,20},{1,9},{5... | collective-permute-start | bytes 49160 | tf_op jit(solution)/shard_map/ppermute | solution.py:49
  61.8 6.2 %collective-permute-start.4 = (f32[1,6144]{1,0:T(1,128)S(1)}, f32[1,6144]{1,0:T(1,128)S(1)}, u32[]{:S(2)}, u32[]{:S(2)}) collective-permute-start(f32[1,6144]{1,0:T(1,128)S(1)} %row_pass.3), channel_id=1, source_target_pairs={{0,1},{1,0},{2,3},{3,2},{4,5},{5,4},{6,7},{7,6},{8,9},{9,8},{10,11... | collective-permute-start | bytes 73736 | tf_op jit(solution)/shard_map/ppermute | solution.py:49
  62.4 5.6 %collective-permute-start.5 = (f32[1,6144]{1,0:T(1,128)S(1)}, f32[1,6144]{1,0:T(1,128)S(1)}, u32[]{:S(2)}, u32[]{:S(2)}) collective-permute-start(f32[1,6144]{1,0:T(1,128)S(1)} %row_pass.3), channel_id=1, source_target_pairs={{0,2},{1,3},{2,0},{3,1},{4,6},{5,7},{6,4},{7,5},{8,10},{9,11},{10,... | collective-permute-start | bytes 73736 | tf_op jit(solution)/shard_map/ppermute | solution.py:49
  63.9 4.8 %collective-permute-start.6 = (f32[1,6144]{1,0:T(1,128)S(1)}, f32[1,6144]{1,0:T(1,128)S(1)}, u32[]{:S(2)}, u32[]{:S(2)}) collective-permute-start(f32[1,6144]{1,0:T(1,128)S(1)} %row_pass.3), channel_id=1, source_target_pairs={{0,3},{1,2},{2,1},{3,0},{4,7},{5,6},{6,5},{7,4},{8,11},{9,10},{10,... | collective-permute-start | bytes 73736 | tf_op jit(solution)/shard_map/ppermute | solution.py:49
  66.4 15.6 %collective-permute-start.24 = (f32[2,10,32,256]{3,2,1,0:T(8,128)S(1)}, f32[2,10,32,256]{3,2,1,0:T(8,128)S(1)}, u32[]{:S(2)}, u32[]{:S(2)}) collective-permute-start(f32[2,10,32,256]{3,2,1,0:T(8,128)S(1)} %pad_maximum_fusion.1), channel_id=1, source_target_pairs={{0,2},{1,3},{2,0},{3,1},{4,6},{5,7},{6,4},{7,5},{8,10},{9,11},{10,... | collective-permute-start | bytes 1966088 | tf_op jit(solution)/shard_map/ppermute | solution.py:49
  68.8 5.4 %collective-permute-start.7 = (f32[1,6144]{1,0:T(1,128)S(1)}, f32[1,6144]{1,0:T(1,128)S(1)}, u32[]{:S(2)}, u32[]{:S(2)}) collective-permute-start(f32[1,6144]{1,0:T(1,128)S(1)} %add_add_fusion), channel_id=1, source_target_pairs={{0,16},{4,20},{8,24},{12,28},{16,0},{20,4},{24,8},{28,12},{1,17},{... | collective-permute-start | bytes 73736 | tf_op jit(solution)/shard_map/ppermute | solution.py:49
  74.2 1.3 collective-permute-start.8
  74.2 43.1 %collective-permute-start.21 = (f32[1280,256]{1,0:T(8,128)S(1)}, f32[1280,256]{1,0:T(8,128)S(1)}, u32[]{:S(2)}, u32[]{:S(2)}) collective-permute-start(f32[1280,256]{1,0:T(8,128)S(1)} %units.3.unit_ref.own_ref), channel_id=1, source_target_pairs={{0,4},{4,0},{8,12},{12,8},{16,20},{20,16},{24,28},{28,24},{1,5},{5... | collective-permute-start | bytes 3932168 | tf_op jit(solution)/shard_map/ppermute | solution.py:49
  77.5 5.6 %collective-permute-start.9 = (f32[1,4096]{1,0:T(1,128)S(1)}, f32[1,4096]{1,0:T(1,128)S(1)}, u32[]{:S(2)}, u32[]{:S(2)}) collective-permute-start(f32[1,4096]{1,0:T(1,128)S(1)} %column_pass.2.a_ref), channel_id=1, source_target_pairs={{0,8},{4,12},{8,0},{12,4},{16,24},{20,28},{24,16},{28,20},{1,9},{5... | collective-permute-start | bytes 49160 | tf_op jit(solution)/shard_map/ppermute | solution.py:49
  83.0 34.3 %collective-permute-start.25 = (f32[4,10,32,256]{3,2,1,0:T(8,128)S(1)}, f32[4,10,32,256]{3,2,1,0:T(8,128)S(1)}, u32[]{:S(2)}, u32[]{:S(2)}) collective-permute-start(f32[4,10,32,256]{3,2,1,0:T(8,128)S(1)} %pad_maximum_fusion.far_ref), channel_id=1, source_target_pairs={{0,4},{4,0},{8,12},{12,8},{16,20},{20,16},{24,28},{28,24},{1,5},{5... | collective-permute-start | bytes 3932168 | tf_op jit(solution)/shard_map/ppermute | solution.py:49
  84.7 3.7 %collective-permute-start.10 = (f32[1,1024]{1,0:T(1,128)S(1)}, f32[1,1024]{1,0:T(1,128)S(1)}, u32[]{:S(2)}, u32[]{:S(2)}) collective-permute-start(f32[1,1024]{1,0:T(1,128)S(1)} %row_pass.4), channel_id=1, source_target_pairs={{0,1},{1,0},{2,3},{3,2},{4,5},{5,4},{6,7},{7,6},{8,9},{9,8},{10,11... | collective-permute-start | bytes 12296 | tf_op jit(solution)/shard_map/ppermute | solution.py:49
  85.2 3.6 %collective-permute-start.11 = (f32[1,1024]{1,0:T(1,128)S(1)}, f32[1,1024]{1,0:T(1,128)S(1)}, u32[]{:S(2)}, u32[]{:S(2)}) collective-permute-start(f32[1,1024]{1,0:T(1,128)S(1)} %row_pass.4), channel_id=1, source_target_pairs={{0,2},{1,3},{2,0},{3,1},{4,6},{5,7},{6,4},{7,5},{8,10},{9,11},{10,... | collective-permute-start | bytes 12296 | tf_op jit(solution)/shard_map/ppermute | solution.py:49
  86.8 4.5 %collective-permute-start.12 = (f32[1,1024]{1,0:T(1,128)S(1)}, f32[1,1024]{1,0:T(1,128)S(1)}, u32[]{:S(2)}, u32[]{:S(2)}) collective-permute-start(f32[1,1024]{1,0:T(1,128)S(1)} %row_pass.4), channel_id=1, source_target_pairs={{0,3},{1,2},{2,1},{3,0},{4,7},{5,6},{6,5},{7,4},{8,11},{9,10},{10,... | collective-permute-start | bytes 12296 | tf_op jit(solution)/shard_map/ppermute | solution.py:49
  91.3 5.1 %collective-permute-start.13 = (f32[1,1024]{1,0:T(1,128)S(1)}, f32[1,1024]{1,0:T(1,128)S(1)}, u32[]{:S(2)}, u32[]{:S(2)}) collective-permute-start(f32[1,1024]{1,0:T(1,128)S(1)} %add_add_fusion.2), channel_id=1, source_target_pairs={{0,16},{4,20},{8,24},{12,28},{16,0},{20,4},{24,8},{28,12},{1,17},{... | collective-permute-start | bytes 12296 | tf_op jit(solution)/shard_map/ppermute | solution.py:49
  96.4 1.2 collective-permute-start.14
  99.7 3.8 %collective-permute-start.15 = (f32[1,4096]{1,0:T(1,128)S(1)}, f32[1,4096]{1,0:T(1,128)S(1)}, u32[]{:S(2)}, u32[]{:S(2)}) collective-permute-start(f32[1,4096]{1,0:T(1,128)S(1)} %column_pass.3.a_ref), channel_id=1, source_target_pairs={{0,8},{4,12},{8,0},{12,4},{16,24},{20,28},{24,16},{28,20},{1,9},{5... | collective-permute-start | bytes 49160 | tf_op jit(solution)/shard_map/ppermute | solution.py:49
  105.0 3.7 %collective-permute-start.16 = (f32[1,1024]{1,0:T(1,128)S(1)}, f32[1,1024]{1,0:T(1,128)S(1)}, u32[]{:S(2)}, u32[]{:S(2)}) collective-permute-start(f32[1,1024]{1,0:T(1,128)S(1)} %row_pass.5), channel_id=1, source_target_pairs={{0,1},{1,0},{2,3},{3,2},{4,5},{5,4},{6,7},{7,6},{8,9},{9,8},{10,11... | collective-permute-start | bytes 12296 | tf_op jit(solution)/shard_map/ppermute | solution.py:49
  106.3 3.6 %collective-permute-start.17 = (f32[1,1024]{1,0:T(1,128)S(1)}, f32[1,1024]{1,0:T(1,128)S(1)}, u32[]{:S(2)}, u32[]{:S(2)}) collective-permute-start(f32[1,1024]{1,0:T(1,128)S(1)} %row_pass.5), channel_id=1, source_target_pairs={{0,2},{1,3},{2,0},{3,1},{4,6},{5,7},{6,4},{7,5},{8,10},{9,11},{10,... | collective-permute-start | bytes 12296 | tf_op jit(solution)/shard_map/ppermute | solution.py:49
  107.1 4.5 %collective-permute-start.18 = (f32[1,1024]{1,0:T(1,128)S(1)}, f32[1,1024]{1,0:T(1,128)S(1)}, u32[]{:S(2)}, u32[]{:S(2)}) collective-permute-start(f32[1,1024]{1,0:T(1,128)S(1)} %row_pass.5), channel_id=1, source_target_pairs={{0,3},{1,2},{2,1},{3,0},{4,7},{5,6},{6,5},{7,4},{8,11},{9,10},{10,... | collective-permute-start | bytes 12296 | tf_op jit(solution)/shard_map/ppermute | solution.py:49
  111.6 4.6 %collective-permute-start.19 = (f32[1,1024]{1,0:T(1,128)S(1)}, f32[1,1024]{1,0:T(1,128)S(1)}, u32[]{:S(2)}, u32[]{:S(2)}) collective-permute-start(f32[1,1024]{1,0:T(1,128)S(1)} %add_add_fusion.1), channel_id=1, source_target_pairs={{0,16},{4,20},{8,24},{12,28},{16,0},{20,4},{24,8},{28,12},{1,17},{... | collective-permute-start | bytes 12296 | tf_op jit(solution)/shard_map/ppermute | solution.py:49
  116.2 1.2 collective-permute-start.20
  127.7 55.0 %collective-permute-start.44 = (f32[128,512]{1,0:T(8,128)}, f32[128,512]{1,0:T(8,128)S(1)}, u32[]{:S(2)}, u32[]{:S(2)}) collective-permute-start(f32[128,512]{1,0:T(8,128)} %get-tuple-element.54), channel_id=1, source_target_pairs={{0,8},{4,12},{8,0},{12,4},{16,24},{20,28},{24,16},{28,20},{1,9},{5... | collective-permute-start | bytes 786440 | tf_op jit(solution)/shard_map/ppermute | solution.py:49
  169.8 11.3 %copy-start.16 = (f32[128,1024]{1,0:T(8,128)S(1)}, f32[128,1024]{1,0:T(8,128)}, u32[]{:S(2)}) copy-start(f32[128,1024]{1,0:T(8,128)} %get-tuple-element.56) | copy-start | bytes 1572868
  169.8 13.0 %copy-start.13 = (f32[128,512]{1,0:T(8,128)S(1)}, f32[128,512]{1,0:T(8,128)}, u32[]{:S(2)}) copy-start(f32[128,512]{1,0:T(8,128)} %get-tuple-element.53) | copy-start | bytes 786436
  178.8 12.6 %collective-permute-start.26 = (f32[136,512]{1,0:T(8,128)}, f32[136,512]{1,0:T(8,128)S(1)}, u32[]{:S(2)}, u32[]{:S(2)}) collective-permute-start(f32[136,512]{1,0:T(8,128)} %get-tuple-element.46), channel_id=1, source_target_pairs={{0,8},{4,12},{8,0},{12,4},{16,24},{20,28},{24,16},{28,20},{1,9},{5... | collective-permute-start | bytes 835592 | tf_op jit(solution)/shard_map/ppermute | solution.py:49
  180.6 39.9 %copy-start.15 = (f32[128,1024]{1,0:T(8,128)S(1)}, f32[128,1024]{1,0:T(8,128)}, u32[]{:S(2)}) copy-start(f32[128,1024]{1,0:T(8,128)} %get-tuple-element.52) | copy-start | bytes 1572868
  180.6 43.6 %copy-start.14 = (f32[4,10,32,256]{3,2,1,0:T(8,128)S(1)}, f32[4,10,32,256]{3,2,1,0:T(8,128)}, u32[]{:S(2)}) copy-start(f32[4,10,32,256]{3,2,1,0:T(8,128)} %get-tuple-element.48) | copy-start | bytes 3932164
  180.6 44.3 %copy-start.12 = (f32[128,1024]{1,0:T(8,128)S(1)}, f32[128,1024]{1,0:T(8,128)}, u32[]{:S(2)}) copy-start(f32[128,1024]{1,0:T(8,128)} %get-tuple-element.57) | copy-start | bytes 1572868
  180.7 44.1 %collective-permute-start.52 = (f32[128,1024]{1,0:T(8,128)S(1)}, f32[128,1024]{1,0:T(8,128)S(1)}, u32[]{:S(2)}, u32[]{:S(2)}) collective-permute-start(f32[128,1024]{1,0:T(8,128)S(1)} %copy-done.17), channel_id=1, source_target_pairs={{0,8},{4,12},{8,0},{12,4},{16,24},{20,28},{24,16},{28,20},{1,9},{5... | collective-permute-start | bytes 1572872 | tf_op jit(solution)/shard_map/ppermute | solution.py:49
  181.0 44.0 %collective-permute-start.48 = (f32[128,1024]{1,0:T(8,128)S(1)}, f32[128,1024]{1,0:T(8,128)S(1)}, u32[]{:S(2)}, u32[]{:S(2)}) collective-permute-start(f32[128,1024]{1,0:T(8,128)S(1)} %copy-done.16), channel_id=1, source_target_pairs={{0,8},{4,12},{8,0},{12,4},{16,24},{20,28},{24,16},{28,20},{1,9},{5... | collective-permute-start | bytes 1572872 | tf_op jit(solution)/shard_map/ppermute | solution.py:49
  182.8 36.2 %collective-permute-start.46 = (f32[64,512]{1,0:T(8,128)S(1)}, f32[64,512]{1,0:T(8,128)S(1)}, u32[]{:S(2)}, u32[]{:S(2)}) collective-permute-start(f32[64,512]{1,0:T(8,128)S(1)} %slice_add_fusion.11), channel_id=1, source_target_pairs={{0,16},{4,20},{8,24},{12,28},{16,0},{20,4},{24,8},{28,12},{1,17},{... | collective-permute-start | bytes 393224 | tf_op jit(solution)/shard_map/ppermute | solution.py:49
  192.4 33.1 %copy-start.10 = (f32[128,1024]{1,0:T(8,128)S(1)}, f32[128,1024]{1,0:T(8,128)}, u32[]{:S(2)}) copy-start(f32[128,1024]{1,0:T(8,128)} %get-tuple-element.55) | copy-start | bytes 1572868
  192.4 23.1 %collective-permute-start.27 = (f32[72,512]{1,0:T(8,128)S(1)}, f32[72,512]{1,0:T(8,128)S(1)}, u32[]{:S(2)}, u32[]{:S(2)}) collective-permute-start(f32[72,512]{1,0:T(8,128)S(1)} %slice_add_fusion.6), channel_id=1, source_target_pairs={{0,16},{4,20},{8,24},{12,28},{16,0},{20,4},{24,8},{28,12},{1,17},{... | collective-permute-start | bytes 442376 | tf_op jit(solution)/shard_map/ppermute | solution.py:49
  215.6 1.3 collective-permute-start.28
  216.9 3.6 %collective-permute-start.29 = (f32[1,128]{1,0:T(1,128)S(1)}, f32[1,128]{1,0:T(1,128)S(1)}, u32[]{:S(2)}, u32[]{:S(2)}) collective-permute-start(f32[1,128]{1,0:T(1,128)S(1)} %slice_add_fusion.19), channel_id=1, source_target_pairs={{0,1},{1,0},{2,3},{3,2},{4,5},{5,4},{6,7},{7,6},{8,9},{9,8},{10,11... | collective-permute-start | bytes 1544 | tf_op jit(solution)/shard_map/ppermute | solution.py:49
  217.5 6.8 %collective-permute-start.30 = (f32[1,128]{1,0:T(1,128)S(1)}, f32[1,128]{1,0:T(1,128)S(1)}, u32[]{:S(2)}, u32[]{:S(2)}) collective-permute-start(f32[1,128]{1,0:T(1,128)S(1)} %slice_add_fusion.19), channel_id=1, source_target_pairs={{0,2},{1,3},{2,0},{3,1},{4,6},{5,7},{6,4},{7,5},{8,10},{9,11},{10,... | collective-permute-start | bytes 1544 | tf_op jit(solution)/shard_map/ppermute | solution.py:49
  219.0 5.3 %collective-permute-start.31 = (f32[1,128]{1,0:T(1,128)S(1)}, f32[1,128]{1,0:T(1,128)S(1)}, u32[]{:S(2)}, u32[]{:S(2)}) collective-permute-start(f32[1,128]{1,0:T(1,128)S(1)} %slice_add_fusion.19), channel_id=1, source_target_pairs={{0,3},{1,2},{2,1},{3,0},{4,7},{5,6},{6,5},{7,4},{8,11},{9,10},{10,... | collective-permute-start | bytes 1544 | tf_op jit(solution)/shard_map/ppermute | solution.py:49
  220.5 15.2 %collective-permute-start.39 = (f32[128,1024]{1,0:T(8,128)S(1)}, f32[128,1024]{1,0:T(8,128)S(1)}, u32[]{:S(2)}, u32[]{:S(2)}) collective-permute-start(f32[128,1024]{1,0:T(8,128)S(1)} %copy-done.15), channel_id=1, source_target_pairs={{0,8},{4,12},{8,0},{12,4},{16,24},{20,28},{24,16},{28,20},{1,9},{5... | collective-permute-start | bytes 1572872 | tf_op jit(solution)/shard_map/ppermute | solution.py:49
  224.2 25.0 %collective-permute-start.35 = (f32[4,10,32,256]{3,2,1,0:T(8,128)}, f32[4,10,32,256]{3,2,1,0:T(8,128)S(1)}, u32[]{:S(2)}, u32[]{:S(2)}) collective-permute-start(f32[4,10,32,256]{3,2,1,0:T(8,128)} %get-tuple-element.50), channel_id=1, source_target_pairs={{0,4},{4,0},{8,12},{12,8},{16,20},{20,16},{24,28},{28,24},{1,5},{5... | collective-permute-start | bytes 3932168 | tf_op jit(solution)/shard_map/ppermute | solution.py:49
  224.2 28.3 %collective-permute-start.32 = (f32[4,10,32,256]{3,2,1,0:T(8,128)S(1)}, f32[4,10,32,256]{3,2,1,0:T(8,128)S(1)}, u32[]{:S(2)}, u32[]{:S(2)}) collective-permute-start(f32[4,10,32,256]{3,2,1,0:T(8,128)S(1)} %copy-done.14), channel_id=1, source_target_pairs={{0,4},{4,0},{8,12},{12,8},{16,20},{20,16},{24,28},{28,24},{1,5},{5... | collective-permute-start | bytes 3932168 | tf_op jit(solution)/shard_map/ppermute | solution.py:49
  224.8 48.1 %collective-permute-start.45 = (f32[32,512]{1,0:T(8,128)S(1)}, f32[32,512]{1,0:T(8,128)S(1)}, u32[]{:S(2)}, u32[]{:S(2)}) collective-permute-start(f32[32,512]{1,0:T(8,128)S(1)} %get-tuple-element.69), channel_id=1, source_target_pairs={{0,4},{4,0},{8,12},{12,8},{16,20},{20,16},{24,28},{28,24},{1,5},{5... | collective-permute-start | bytes 196616 | tf_op jit(solution)/shard_map/ppermute | solution.py:49
  225.0 12.1 %copy-start.11 = (f32[128,1024]{1,0:T(8,128)S(1)}, f32[128,1024]{1,0:T(8,128)}, u32[]{:S(2)}) copy-start(f32[128,1024]{1,0:T(8,128)} %get-tuple-element.51) | copy-start | bytes 1572868
  225.0 48.5 %collective-permute-start.47 = (f32[32,512]{1,0:T(8,128)S(1)}, f32[32,512]{1,0:T(8,128)S(1)}, u32[]{:S(2)}, u32[]{:S(2)}) collective-permute-start(f32[32,512]{1,0:T(8,128)S(1)} %get-tuple-element.79), channel_id=1, source_target_pairs={{0,4},{4,0},{8,12},{12,8},{16,20},{20,16},{24,28},{28,24},{1,5},{5... | collective-permute-start | bytes 196616 | tf_op jit(solution)/shard_map/ppermute | solution.py:49
  225.6 26.7 %copy-start.9 = (f32[4,10,32,256]{3,2,1,0:T(8,128)S(1)}, f32[4,10,32,256]{3,2,1,0:T(8,128)}, u32[]{:S(2)}) copy-start(f32[4,10,32,256]{3,2,1,0:T(8,128)} %get-tuple-element.49) | copy-start | bytes 3932164
  235.7 13.5 %collective-permute-start.54 = (f32[64,1024]{1,0:T(8,128)S(1)}, f32[64,1024]{1,0:T(8,128)S(1)}, u32[]{:S(2)}, u32[]{:S(2)}) collective-permute-start(f32[64,1024]{1,0:T(8,128)S(1)} %slice_add_fusion.3), channel_id=1, source_target_pairs={{0,16},{4,20},{8,24},{12,28},{16,0},{20,4},{24,8},{28,12},{1,17},{... | collective-permute-start | bytes 786440 | tf_op jit(solution)/shard_map/ppermute | solution.py:49
  249.2 18.1 %collective-permute-start.50 = (f32[64,1024]{1,0:T(8,128)S(1)}, f32[64,1024]{1,0:T(8,128)S(1)}, u32[]{:S(2)}, u32[]{:S(2)}) collective-permute-start(f32[64,1024]{1,0:T(8,128)S(1)} %slice_add_fusion.4), channel_id=1, source_target_pairs={{0,16},{4,20},{8,24},{12,28},{16,0},{20,4},{24,8},{28,12},{1,17},{... | collective-permute-start | bytes 786440 | tf_op jit(solution)/shard_map/ppermute | solution.py:49
  249.3 23.6 %collective-permute-start.41 = (f32[64,1024]{1,0:T(8,128)S(1)}, f32[64,1024]{1,0:T(8,128)S(1)}, u32[]{:S(2)}, u32[]{:S(2)}) collective-permute-start(f32[64,1024]{1,0:T(8,128)S(1)} %slice_add_fusion.5), channel_id=1, source_target_pairs={{0,16},{4,20},{8,24},{12,28},{16,0},{20,4},{24,8},{28,12},{1,17},{... | collective-permute-start | bytes 786440 | tf_op jit(solution)/shard_map/ppermute | solution.py:49
  252.6 21.0 %collective-permute-start.36 = (f32[2,1,10,32,256]{4,3,2,1,0:T(8,128)S(1)}, f32[2,1,10,32,256]{4,3,2,1,0:T(8,128)S(1)}, u32[]{:S(2)}, u32[]{:S(2)}) collective-permute-start(f32[2,1,10,32,256]{4,3,2,1,0:T(8,128)S(1)} %slice.236), channel_id=1, source_target_pairs={{0,1},{1,0},{2,3},{3,2},{4,5},{5,4},{6,7},{7,6},{8,9},{9,8},{10,11... | collective-permute-start | bytes 1966088 | tf_op jit(solution)/shard_map/ppermute | solution.py:49
  267.3 17.6 %collective-permute-start.33 = (f32[1,2,10,32,256]{4,3,2,1,0:T(8,128)S(1)}, f32[1,2,10,32,256]{4,3,2,1,0:T(8,128)S(1)}, u32[]{:S(2)}, u32[]{:S(2)}) collective-permute-start(f32[1,2,10,32,256]{4,3,2,1,0:T(8,128)S(1)} %slice_bitcast_fusion), channel_id=1, source_target_pairs={{0,2},{1,3},{2,0},{3,1},{4,6},{5,7},{6,4},{7,5},{8,10},{9,11},{10,... | collective-permute-start | bytes 1966088 | tf_op jit(solution)/shard_map/ppermute | solution.py:49
  272.9 1.3 collective-permute-start.53
  272.9 1.5 collective-permute-start.49
  273.5 1.3 collective-permute-start.55
  273.6 1.4 collective-permute-start.51
  274.2 16.8 %collective-permute-start.43 = (f32[32,512]{1,0:T(8,128)S(1)}, f32[32,512]{1,0:T(8,128)S(1)}, u32[]{:S(2)}, u32[]{:S(2)}) collective-permute-start(f32[32,512]{1,0:T(8,128)S(1)} %get-tuple-element.67), channel_id=1, source_target_pairs={{0,4},{4,0},{8,12},{12,8},{16,20},{20,16},{24,28},{28,24},{1,5},{5... | collective-permute-start | bytes 196616 | tf_op jit(solution)/shard_map/ppermute | solution.py:49
  274.5 16.6 %collective-permute-start.40 = (f32[32,1024]{1,0:T(8,128)S(1)}, f32[32,1024]{1,0:T(8,128)S(1)}, u32[]{:S(2)}, u32[]{:S(2)}) collective-permute-start(f32[32,1024]{1,0:T(8,128)S(1)} %get-tuple-element.65), channel_id=1, source_target_pairs={{0,4},{4,0},{8,12},{12,8},{16,20},{20,16},{24,28},{28,24},{1,5},{5... | collective-permute-start | bytes 393224 | tf_op jit(solution)/shard_map/ppermute | solution.py:49
  274.8 16.2 %collective-permute-start.42 = (f32[32,1024]{1,0:T(8,128)S(1)}, f32[32,1024]{1,0:T(8,128)S(1)}, u32[]{:S(2)}, u32[]{:S(2)}) collective-permute-start(f32[32,1024]{1,0:T(8,128)S(1)} %get-tuple-element.75), channel_id=1, source_target_pairs={{0,4},{4,0},{8,12},{12,8},{16,20},{20,16},{24,28},{28,24},{1,5},{5... | collective-permute-start | bytes 393224 | tf_op jit(solution)/shard_map/ppermute | solution.py:49
  275.0 15.9 %collective-permute-start.37 = (f32[1,1,10,32,256]{4,3,2,1,0:T(8,128)S(1)}, f32[1,1,10,32,256]{4,3,2,1,0:T(8,128)S(1)}, u32[]{:S(2)}, u32[]{:S(2)}) collective-permute-start(f32[1,1,10,32,256]{4,3,2,1,0:T(8,128)S(1)} %slice.238), channel_id=1, source_target_pairs={{0,2},{1,3},{2,0},{3,1},{4,6},{5,7},{6,4},{7,5},{8,10},{9,11},{10,... | collective-permute-start | bytes 983048 | tf_op jit(solution)/shard_map/ppermute | solution.py:49
  285.1 7.7 %collective-permute-start.34 = (f32[1,1,10,32,256]{4,3,2,1,0:T(8,128)S(1)}, f32[1,1,10,32,256]{4,3,2,1,0:T(8,128)S(1)}, u32[]{:S(2)}, u32[]{:S(2)}) collective-permute-start(f32[1,1,10,32,256]{4,3,2,1,0:T(8,128)S(1)} %slice.234), channel_id=1, source_target_pairs={{0,1},{1,0},{2,3},{3,2},{4,5},{5,4},{6,7},{7,6},{8,9},{9,8},{10,11... | collective-permute-start | bytes 983048 | tf_op jit(solution)/shard_map/ppermute | solution.py:49
  291.0 16.6 %collective-permute-start.38 = (f32[10,32,256]{2,1,0:T(8,128)S(1)}, f32[10,32,256]{2,1,0:T(8,128)S(1)}, u32[]{:S(2)}, u32[]{:S(2)}) collective-permute-start(f32[10,32,256]{2,1,0:T(8,128)S(1)} %fusion.1), channel_id=1, source_target_pairs={{0,16},{4,20},{8,24},{12,28},{16,0},{20,4},{24,8},{28,12},{1,17},{... | collective-permute-start | bytes 983048 | tf_op jit(solution)/shard_map/ppermute | solution.py:49
  (10 other events, 27.2 us)
where the time goes:
time: 311 us; the launch traced here: 310 us
  waiting for transfers between devices  138 us (44%)
  Pallas kernels  98 us (32%)
  starting transfers between devices  59.5 us (19%)
  local copies, waits for them, and re-layouts  6.15 us (2%)
  other arithmetic  5.37 us (2%)
    ppermute x56, waiting for transfers between devices, exchange(): return lax.ppermute(value, axis, [(i, i ^ mask) for i in range(size)])  138 us
    ppermute x56, starting transfers between devices, exchange(): return lax.ppermute(value, axis, [(i, i ^ mask) for i in range(size)])  59.5 us
    pallas_call x5, Pallas kernels, gradients(): pl.pallas_call(kernel, grid_spec=pltpu.PrefetchScalarGridSpec(num_scalar_...  59.3 us
    pallas_call x1, Pallas kernels, row_sums(): pl.pallas_call(kernel, grid=(steps,), in_specs=[SCALARS, pl.BlockSpec((ro...  17.3 us
  transfers between devices with their start and end apart: 56, of which 28 were waited for; matrix products, arithmetic and copies ran while one was open for 2% of the time, Pallas kernels for 28%

commit v1 on v0

--- a/solution.py
+++ b/solution.py
@@ -20,7 +20,6 @@
 LOG2E = math.log2(math.e)
 
 CHUNKS = (1, 2, 2, 2, 1)
-LOSS_ROWS = 8
 MIB = 1 << 20
 F32 = jnp.float32
 BF16 = jnp.bfloat16
@@ -157,14 +156,20 @@
 
     def kernel(place_ref, *refs):
         parts = refs[: len(gathered)]
-        proto_ref, mass_ref, sum_ref, rows_ref = refs[len(gathered) :]
+        proto_ref, mass_ref, sum_ref, rows_ref, parts_ref, sem_ref = refs[len(gathered) :]
         step = pl.program_id(0)
 
         @pl.when(step == 0)
         def _():
-            for j, part in enumerate(parts):
+            copies = [
+                pltpu.make_async_copy(part, parts_ref.at[j], sem_ref.at[j]) for j, part in enumerate(parts)
+            ]
+            for copy in copies:
+                copy.start()
+            for j, copy in enumerate(copies):
+                copy.wait()
                 start = pl.multiple_of((place_ref[0] ^ j) * part_rows, part_rows)
-                rows_ref[pl.ds(start, part_rows)] = part[...].astype(BF16)
+                rows_ref[pl.ds(start, part_rows)] = parts_ref[j].astype(BF16)
 
         at = pl.multiple_of(step * width, width)
         part = min(512, width)
@@ -181,10 +186,14 @@
         grid_spec=pltpu.PrefetchScalarGridSpec(
             num_scalar_prefetch=1,
             grid=(steps,),
-            in_specs=[pl.BlockSpec((part_rows, dim), lambda i, s: (0, 0)) for _ in gathered]
+            in_specs=[pl.BlockSpec(memory_space=pl.ANY)] * len(gathered)
             + [pl.BlockSpec((dim, width), lambda i, s: (0, s[0] * steps + i))],
             out_specs=[WHOLE, pl.BlockSpec((1, width), lambda i, s: (0, i))],
-            scratch_shapes=[pltpu.VMEM((rows, dim), BF16)],
+            scratch_shapes=[
+                pltpu.VMEM((rows, dim), BF16),
+                pltpu.VMEM((len(gathered), part_rows, dim), F32),
+                pltpu.SemaphoreType.DMA((len(gathered),)),
+            ],
         ),
         out_shape=[vmem((rows, columns), F32), jax.ShapeDtypeStruct((1, columns), F32)],
         compiler_params=params(),
@@ -329,7 +338,6 @@
     crops, images, pieces, blocks, factor, order = geometry
     dim = protos.shape[0]
     half = dim // 2
-    out_rows = half + (LOSS_ROWS if last else 0)
     row_count = rows.shape[0]
     teacher_rows, columns = mass.shape
     groups = teacher_rows // (2 * images)
@@ -351,8 +359,8 @@
         send_ref, keep_ref = refs[:2]
         refs = refs[2:]
         if last:
-            wing_refs = refs[:4]
-            refs = refs[4:]
+            wing_refs, loss_ref = refs[:4], refs[4]
+            refs = refs[5:]
             sem_ref = refs.pop()
             feat_ref, targ_ref = feat_in, targ_in
         else:
@@ -456,13 +464,12 @@
                 total = total + targ_ref[tbase + images : tbase + 2 * images] * (crop_rows[0] + shared)
             product = jnp.sum(jnp.sum(total, axis=0, keepdims=True), axis=1, keepdims=True)
             loss = norm_ref[:, :1] * (1.0 / (4 * pieces)) - product * (1.0 / (factor * STUDENT_TEMP))
-            keep_ref[half:] = loss + jnp.zeros((LOSS_ROWS, width), F32)
-            send_ref[half:] = loss + jnp.zeros((LOSS_ROWS, width), F32)
+            loss_ref[...] = loss + jnp.zeros((1, 128), F32)
             for copy in copies:
                 copy.wait()
 
-    out_shape = [hbm((out_rows, steps * width), F32)] * 2
-    out_specs = [pl.BlockSpec((out_rows, width), lambda i, s: (0, i))] * 2
+    out_shape = [hbm((half, steps * width), F32)] * 2
+    out_specs = [pl.BlockSpec((half, width), lambda i, s: (0, i))] * 2
     operands = [protos, mass, column_sums, row_sum, rows, cols, offsets]
     in_specs = [
         pl.BlockSpec((dim, width), lambda i, s: (0, s[0] * total_steps + s[3] + i)),
@@ -477,8 +484,8 @@
         in_specs += [WHOLE] * 2
     if last:
         shape = (pieces, crops, piece_images, dim)
-        out_shape = out_shape + [hbm(shape, F32)] * 4
-        out_specs = out_specs + [pl.BlockSpec(memory_space=pl.ANY)] * 4
+        out_shape = out_shape + [hbm(shape, F32)] * 4 + [jax.ShapeDtypeStruct((1, 128), F32)]
+        out_specs = out_specs + [pl.BlockSpec(memory_space=pl.ANY)] * 4 + [WHOLE]
     else:
         out_shape = out_shape + [vmem((groups, crops, images, dim), F32), vmem((teacher_rows, dim), F32)]
         out_specs = out_specs + [WHOLE] * 2
@@ -652,13 +659,12 @@
         )
         send, keep = outs[:2]
         carried = outs[2:]
-        loss_rows = LOSS_ROWS if chunk == len(CHUNKS) - 1 else 0
         for bit in middle[:-1]:
             keep = keep + swap(send, BATCH, bit)
-            end = keep.shape[0] - loss_rows
+            end = keep.shape[0]
             send = keep[end // 2 :]
-            keep = jnp.concatenate([keep[: end // 2], keep[end:]], axis=0)
-        half = (keep.shape[0] - loss_rows) // 2
+            keep = keep[: end // 2]
+        half = keep.shape[0] // 2
         quarter = half // 2
         received = swap(send, BATCH, middle[-1])
         far_send = keep[half:] + received[half:]
@@ -667,18 +673,13 @@
         far_half = swap(far_send, BATCH, top)
         near_core = swap(near_core, BATCH, core)
         far_core = far_half[quarter:half]
-        if loss_rows:
-            loss = far_send[half:] + far_half[half:]
-            far_core = jnp.concatenate([far_core, loss], axis=0)
         far_core = swap(far_core, BATCH, core)
-        if loss_rows:
-            loss = (loss + far_core[quarter:])[:1, :128]
-        pieces.append([near_own, near_core, far_half[:quarter], far_core[:quarter]])
+        pieces.append([near_own, near_core, far_half[:quarter], far_core])
     early = len(CHUNKS) - 2
     grad_prototypes = assemble(places, pieces[:early], 0, None)
     grad_prototypes = assemble(places, pieces[early:], early, grad_prototypes)
 
-    far_wings, near_wings = carried[:2], carried[2:]
+    far_wings, near_wings, loss = carried[:2], carried[2:4], carried[4]
     received = [swap(far_wings[1], BATCH, core)]
     received = [swap(far_wings[0], BATCH, core)] + received
     totals = []
@@ -695,6 +696,8 @@
     received = swap(totals[1], BATCH, top)
     grad_features = finish(totals[0], received, unit_own, raw_own)
 
+    received = swap(loss, BATCH, core)
+    loss = bits_sum(loss + received, BATCH, range(1, batch_bits))
     loss = bits_sum(loss, PROTO, range(proto_bits))
     mean_loss = loss[0, 0] / (images_all * PAIRS)
     return (mean_loss, grad_features, grad_prototypes)

time: 311 us -> 319 us (1.026)
  waiting for transfers between devices: 138 us -> 149 us
    ppermute x56 -> x60, waiting for transfers between devices: 138 us -> 149 us  [exchange(): return lax.ppermute(value, axis, [(i, i ^ mask) for i in range(size)])]
    ppermute x56 -> x60, starting transfers between devices: 59.5 us -> 58.2 us  [exchange(): return lax.ppermute(value, axis, [(i, i ^ mask) for i in range(size)])]
  transfers between devices with their start and end apart: 56 -> 60, of which waited for: 28 -> 30; matrix products, arithmetic and copies ran while one was open for 2% -> 1% of each run, Pallas kernels for 28% -> 11%
where the time goes in v1:
time: 319 us; the launch traced here: 318 us
  waiting for transfers between devices  149 us (47%)
  Pallas kernels  98.3 us (31%)
  starting transfers between devices  58.2 us (18%)
  local copies, waits for them, and re-layouts  6.11 us (2%)
  other arithmetic  4.48 us (1%)
    ppermute x60, waiting for transfers between devices, exchange(): return lax.ppermute(value, axis, [(i, i ^ mask) for i in range(size)])  149 us
    pallas_call x5, Pallas kernels, gradients(): pl.pallas_call(kernel, grid_spec=pltpu.PrefetchScalarGridSpec(num_scalar_...  59.3 us
    ppermute x60, starting transfers between devices, exchange(): return lax.ppermute(value, axis, [(i, i ^ mask) for i in range(size)])  58.2 us
    pallas_call x1, Pallas kernels, row_sums(): pl.pallas_call(kernel, grid=(steps,), in_specs=[SCALARS, pl.BlockSpec((ro...  17.3 us
  transfers between devices with their start and end apart: 60, of which 30 were waited for; matrix products, arithmetic and copies ran while one was open for 1% of the time, Pallas kernels for 11%

profile of v1, /device:TPU:0, one launch (start us, length us, event | category | flops | bytes accessed | tf_op | source)
XLA Modules:
  0.0 318.1 jit_solution(3023157975796160828)
XLA Ops:
  1.7 4.1 %collective-permute-start.1 = (f32[256,256]{1,0:T(8,128)S(1)}, f32[256,256]{1,0:T(8,128)S(1)}, u32[]{:S(2)}, u32[]{:S(2)}) collective-permute-start(f32[256,256]{1,0:T(8,128)S(1)} %units.2.refs_0_), channel_id=1, source_target_pairs={{0,16},{4,20},{8,24},{12,28},{16,0},{20,4},{24,8},{28,12},{1,17},{... | collective-permute-start | bytes 786440 | tf_op jit(solution)/shard_map/ppermute | solution.py:48
  6.1 1.0 collective-permute-start.22
  7.2 18.4 %collective-permute-done.1.refs_2_ = f32[256,256]{1,0:T(8,128)S(1)} collective-permute-done((f32[256,256]{1,0:T(8,128)S(1)}, f32[256,256]{1,0:T(8,128)S(1)}, u32[]{:S(2)}, u32[]{:S(2)}) %collective-permute-start.1) | collective-permute-done | bytes 262176 | tf_op jit(solution)/shard_map/ppermute | solution.py:48
  26.4 5.5 %collective-permute-done.22 = f32[10,32,256]{2,1,0:T(8,128)} collective-permute-done((f32[10,32,256]{2,1,0:T(8,128)S(1)}, f32[10,32,256]{2,1,0:T(8,128)}, u32[]{:S(2)}, u32[]{:S(2)}) %collective-permute-start.22) | collective-permute-done | bytes 327712 | tf_op jit(solution)/shard_map/ppermute | solution.py:48
  31.9 1.5 collective-permute-start.23
  37.0 6.2 %teacher_mass.1 = (f32[1024,4096]{1,0:T(8,128)S(1)}, f32[1,4096]{1,0:T(1,128)S(1)}) custom-call(s32[3]{0:T(128)S(1)} %pad_add_fusion.2.place_ref, f32[256,256]{1,0:T(8,128)S(1)} %copy-done.2, f32[256,256]{1,0:T(8,128)S(1)} %copy-done.6, f32[256,256]{1,0:T(8,128)S(1)} %copy-done.4, f32[256,256]{1,0:T(8,128)} %collective-permute-done.2.refs_3_, ...), custom_call_target="tpu_custom_call" | custom-call | flops 5000000000 | bytes 5000000 | tf_op jit(solution)/shard_map/teacher_mass/pallas_call | solution.py:184
  43.8 17.3 %row_sums.1.refs_0_ = f32[1,5120]{1,0:T(1,128)S(1)} custom-call(s32[3]{0:T(128)S(1)} %pad_add_fusion.2.place_ref, f32[1280,256]{1,0:T(8,128)S(1)} %units.3.unit_ref.own_ref, bf16[256,16384]{1,0:T(8,128)(2,1)} %refs_0_.9), custom_call_target="tpu_custom_call" | custom-call | flops 15000000512 | bytes 15000000 | tf_op jit(solution)/shard_map/row_sums/pallas_call | solution.py:135
  61.2 1.5 row_pass.3
  63.2 1.5 collective-permute-start.5
  64.8 1.4 collective-permute-start.6
  66.2 1.0 pad_maximum_fusion.1
  67.2 1.6 collective-permute-start.24
  69.6 3.6 %collective-permute-start.7 = (f32[1,6144]{1,0:T(1,128)S(1)}, f32[1,6144]{1,0:T(1,128)S(1)}, u32[]{:S(2)}, u32[]{:S(2)}) collective-permute-start(f32[1,6144]{1,0:T(1,128)S(1)} %add_add_fusion), channel_id=1, source_target_pairs={{0,16},{4,20},{8,24},{12,28},{16,0},{20,4},{24,8},{28,12},{1,17},{... | collective-permute-start | bytes 73736 | tf_op jit(solution)/shard_map/ppermute | solution.py:48
  73.2 1.8 collective-permute-done.7
  76.3 1.9 column_pass.2.a_ref
  79.1 3.7 %collective-permute-done.24 = f32[2,10,32,256]{3,2,1,0:T(8,128)S(1)} collective-permute-done((f32[2,10,32,256]{3,2,1,0:T(8,128)S(1)}, f32[2,10,32,256]{3,2,1,0:T(8,128)S(1)}, u32[]{:S(2)}, u32[]{:S(2)}) %collective-permute-start.24) | collective-permute-done | bytes 655392 | tf_op jit(solution)/shard_map/ppermute | solution.py:48
  82.8 1.1 pad_maximum_fusion.far_ref
  84.0 1.5 row_pass.4
  86.0 1.5 collective-permute-start.11
  87.6 1.4 collective-permute-start.12
  89.6 2.4 collective-permute-done.12
  92.1 3.6 %collective-permute-start.13 = (f32[1,1024]{1,0:T(1,128)S(1)}, f32[1,1024]{1,0:T(1,128)S(1)}, u32[]{:S(2)}, u32[]{:S(2)}) collective-permute-start(f32[1,1024]{1,0:T(1,128)S(1)} %add_add_fusion.2), channel_id=1, source_target_pairs={{0,16},{4,20},{8,24},{12,28},{16,0},{20,4},{24,8},{28,12},{1,17},{... | collective-permute-start | bytes 12296 | tf_op jit(solution)/shard_map/ppermute | solution.py:48
  95.6 1.6 collective-permute-done.13
  97.2 1.2 collective-permute-done.14.b_ref
  98.4 1.9 column_pass.3.a_ref
  100.7 3.4 %collective-permute-done.15.b_ref = f32[1,4096]{1,0:T(1,128)S(1)} collective-permute-done((f32[1,4096]{1,0:T(1,128)S(1)}, f32[1,4096]{1,0:T(1,128)S(1)}, u32[]{:S(2)}, u32[]{:S(2)}) %collective-permute-start.15) | collective-permute-done | bytes 16416 | tf_op jit(solution)/shard_map/ppermute | solution.py:48
  104.1 1.5 row_pass.5
  105.5 1.3 collective-permute-start.16
  107.6 1.5 collective-permute-start.18
  109.2 1.2 collective-permute-done.17
  110.4 1.7 collective-permute-done.18
  112.1 3.0 collective-permute-start.19
  115.2 1.5 collective-permute-done.19
  116.7 1.1 row_offsets.1
  117.9 1.8 gather_rows.1
  119.7 8.5 %gradients.5 = (f32[128,512]{1,0:T(8,128)}, f32[128,512]{1,0:T(8,128)}, f32[4,10,128,256]{3,2,1,0:T(8,128)S(1)}, f32[1024,256]{1,0:T(8,128)S(1)}) custom-call(s32[4]{0:T(128)S(1)} %get-tuple-element.61.place_ref, bf16[256,16384]{1,0:T(8,128)(2,1)} %refs_0_.9, f32[1024,4096]{1,0:T(8,128)S(1)} %get-tuple-element.32.mass_ref.refs_1_, ...), custom_call_target="tpu_custom_call" | custom-call | flops 10000000000 | bytes 10000000 | tf_op jit(solution)/shard_map/gradients/pallas_call | solution.py:505
  128.1 13.9 %gradients.6 = (f32[128,1024]{1,0:T(8,128)}, f32[128,1024]{1,0:T(8,128)}, f32[4,10,128,256]{3,2,1,0:T(8,128)S(1)}, f32[1024,256]{1,0:T(8,128)S(1)}) custom-call(s32[4]{0:T(128)S(1)} %get-tuple-element.83.place_ref, bf16[256,16384]{1,0:T(8,128)(2,1)} %refs_0_.9, ...), custom_call_target="tpu_custom_call", output_to_operand_aliasing={{2}: (8, {}), {3}: (9, {})} | custom-call | flops 10000000000 | bytes 10000000 | tf_op jit(solution)/shard_map/gradients/pallas_call | solution.py:505
  142.1 13.7 %gradients.7 = (f32[128,1024]{1,0:T(8,128)}, f32[128,1024]{1,0:T(8,128)}, f32[4,10,128,256]{3,2,1,0:T(8,128)S(1)}, f32[1024,256]{1,0:T(8,128)S(1)}) custom-call(s32[4]{0:T(128)S(1)} %get-tuple-element.84.place_ref, bf16[256,16384]{1,0:T(8,128)(2,1)} %refs_0_.9, ...), custom_call_target="tpu_custom_call", output_to_operand_aliasing={{2}: (8, {}), {3}: (9, {})} | custom-call | flops 10000000000 | bytes 10000000 | tf_op jit(solution)/shard_map/gradients/pallas_call | solution.py:505
  155.8 14.0 %gradients.8 = (f32[128,1024]{1,0:T(8,128)}, f32[128,1024]{1,0:T(8,128)}, f32[4,10,128,256]{3,2,1,0:T(8,128)S(1)}, f32[1024,256]{1,0:T(8,128)S(1)}) custom-call(s32[4]{0:T(128)S(1)} %get-tuple-element.85.place_ref, bf16[256,16384]{1,0:T(8,128)(2,1)} %refs_0_.9, ...), custom_call_target="tpu_custom_call", output_to_operand_aliasing={{2}: (8, {}), {3}: (9, {})} | custom-call | flops 10000000000 | bytes 10000000 | tf_op jit(solution)/shard_map/gradients/pallas_call | solution.py:505
  169.9 9.1 %gradients.9 = (f32[128,512]{1,0:T(8,128)}, f32[128,512]{1,0:T(8,128)}, f32[4,10,32,256]{3,2,1,0:T(8,128)}, f32[4,10,32,256]{3,2,1,0:T(8,128)}, f32[4,10,32,256]...) custom-call(s32[4]{0:T(128)S(1)} %get-tuple-element.86.place_ref, bf16[256,16384]{1,0:T(8,128)(2,1)} %refs_0_.9, ...), custom_call_target="tpu_custom_call" | custom-call | flops 10000000000 | bytes 10000000 | tf_op jit(solution)/shard_map/gradients/pallas_call | solution.py:505
  180.7 2.9 collective-permute-start.28
  183.6 1.1 collective-permute-start.29
  185.4 3.6 %collective-permute-done.29 = f32[1,128]{1,0:T(1,128)S(1)} collective-permute-done((f32[1,128]{1,0:T(1,128)S(1)}, f32[1,128]{1,0:T(1,128)S(1)}, u32[]{:S(2)}, u32[]{:S(2)}) %collective-permute-start.29) | collective-permute-done | bytes 544 | tf_op jit(solution)/shard_map/ppermute | solution.py:48
  189.6 1.5 collective-permute-start.31
  191.1 1.4 collective-permute-start.32
  192.6 2.0 collective-permute-start.52
  195.5 1.1 collective-permute-start.40
  196.9 28.8 %collective-permute-done.44 = f32[128,512]{1,0:T(8,128)S(1)} collective-permute-done((f32[128,512]{1,0:T(8,128)}, f32[128,512]{1,0:T(8,128)S(1)}, u32[]{:S(2)}, u32[]{:S(2)}) %collective-permute-start.44) | collective-permute-done | bytes 262176 | tf_op jit(solution)/shard_map/ppermute | solution.py:48
  226.6 6.4 %collective-permute-done.50 = f32[64,512]{1,0:T(8,128)S(1)} collective-permute-done((f32[64,512]{1,0:T(8,128)S(1)}, f32[64,512]{1,0:T(8,128)S(1)}, u32[]{:S(2)}, u32[]{:S(2)}) %collective-permute-start.50) | collective-permute-done | bytes 131104 | tf_op jit(solution)/shard_map/ppermute | solution.py:48
  233.0 3.4 %collective-permute-start.46 = (f32[64,512]{1,0:T(8,128)S(1)}, f32[64,512]{1,0:T(8,128)S(1)}, u32[]{:S(2)}, u32[]{:S(2)}) collective-permute-start(f32[64,512]{1,0:T(8,128)S(1)} %slice_add_fusion.11), channel_id=1, source_target_pairs={{0,16},{4,20},{8,24},{12,28},{16,0},{20,4},{24,8},{28,12},{1,17},{... | collective-permute-start | bytes 393224 | tf_op jit(solution)/shard_map/ppermute | solution.py:48
  236.4 4.3 %collective-permute-done.46 = f32[64,512]{1,0:T(8,128)S(1)} collective-permute-done((f32[64,512]{1,0:T(8,128)S(1)}, f32[64,512]{1,0:T(8,128)S(1)}, u32[]{:S(2)}, u32[]{:S(2)}) %collective-permute-start.46) | collective-permute-done | bytes 131104 | tf_op jit(solution)/shard_map/ppermute | solution.py:48
  241.6 1.7 collective-permute-start.58
  243.4 13.5 %collective-permute-done.58 = f32[64,1024]{1,0:T(8,128)S(1)} collective-permute-done((f32[64,1024]{1,0:T(8,128)S(1)}, f32[64,1024]{1,0:T(8,128)S(1)}, u32[]{:S(2)}, u32[]{:S(2)}) %collective-permute-start.58) | collective-permute-done | bytes 262176 | tf_op jit(solution)/shard_map/ppermute | solution.py:48
  256.9 3.0 collective-permute-start.42
  261.8 15.5 %collective-permute-done.54 = f32[64,1024]{1,0:T(8,128)S(1)} collective-permute-done((f32[64,1024]{1,0:T(8,128)S(1)}, f32[64,1024]{1,0:T(8,128)S(1)}, u32[]{:S(2)}, u32[]{:S(2)}) %collective-permute-start.54) | collective-permute-done | bytes 262176 | tf_op jit(solution)/shard_map/ppermute | solution.py:48
  277.3 1.3 collective-permute-start.34
  278.6 3.9 %collective-permute-done.42 = f32[64,1024]{1,0:T(8,128)S(1)} collective-permute-done((f32[64,1024]{1,0:T(8,128)S(1)}, f32[64,1024]{1,0:T(8,128)S(1)}, u32[]{:S(2)}, u32[]{:S(2)}) %collective-permute-start.42) | collective-permute-done | bytes 262176 | tf_op jit(solution)/shard_map/ppermute | solution.py:48
  284.6 1.3 collective-permute-start.38
  285.9 1.7 assemble.2.refs_8_
  287.6 7.3 %collective-permute-done.34 = f32[1,2,10,32,256]{4,3,2,1,0:T(8,128)S(1)} collective-permute-done((f32[1,2,10,32,256]{4,3,2,1,0:T(8,128)S(1)}, f32[1,2,10,32,256]{4,3,2,1,0:T(8,128)S(1)}, u32[]{:S(2)}, u32[]{:S(2)}) %collective-permute-start.34) | collective-permute-done | bytes 655392 | tf_op jit(solution)/shard_map/ppermute | solution.py:48
  295.0 5.2 %collective-permute-done.38 = f32[1,1,10,32,256]{4,3,2,1,0:T(8,128)S(1)} collective-permute-done((f32[1,1,10,32,256]{4,3,2,1,0:T(8,128)S(1)}, f32[1,1,10,32,256]{4,3,2,1,0:T(8,128)S(1)}, u32[]{:S(2)}, u32[]{:S(2)}) %collective-permute-start.38) | collective-permute-done | bytes 327712 | tf_op jit(solution)/shard_map/ppermute | solution.py:48
  300.9 1.5 assemble.3
  302.4 5.9 %collective-permute-done.35 = f32[1,1,10,32,256]{4,3,2,1,0:T(8,128)S(1)} collective-permute-done((f32[1,1,10,32,256]{4,3,2,1,0:T(8,128)S(1)}, f32[1,1,10,32,256]{4,3,2,1,0:T(8,128)S(1)}, u32[]{:S(2)}, u32[]{:S(2)}) %collective-permute-start.35) | collective-permute-done | bytes 327712 | tf_op jit(solution)/shard_map/ppermute | solution.py:48
  308.3 7.8 %collective-permute-done.39 = f32[10,32,256]{2,1,0:T(8,128)S(1)} collective-permute-done((f32[10,32,256]{2,1,0:T(8,128)S(1)}, f32[10,32,256]{2,1,0:T(8,128)S(1)}, u32[]{:S(2)}, u32[]{:S(2)}) %collective-permute-start.39) | collective-permute-done | bytes 327712 | tf_op jit(solution)/shard_map/ppermute | solution.py:48
  (159 shorter events, 24.3 us)
Async XLA Ops:
  1.7 23.9 %collective-permute-start.1 = (f32[256,256]{1,0:T(8,128)S(1)}, f32[256,256]{1,0:T(8,128)S(1)}, u32[]{:S(2)}, u32[]{:S(2)}) collective-permute-start(f32[256,256]{1,0:T(8,128)S(1)} %units.2.refs_0_), channel_id=1, source_target_pairs={{0,16},{4,20},{8,24},{12,28},{16,0},{20,4},{24,8},{28,12},{1,17},{... | collective-permute-start | bytes 786440 | tf_op jit(solution)/shard_map/ppermute | solution.py:48
  6.1 25.8 %collective-permute-start.22 = (f32[10,32,256]{2,1,0:T(8,128)S(1)}, f32[10,32,256]{2,1,0:T(8,128)}, u32[]{:S(2)}, u32[]{:S(2)}) collective-permute-start(f32[10,32,256]{2,1,0:T(8,128)S(1)} %constant_dynamic-slice_fusion.1), channel_id=1, source_target_pairs={{0,16},{4,20},{8,24},{12,28},{16,0},{20,4},{24,8},{28,12},{1,17},{... | collective-permute-start | bytes 983048 | tf_op jit(solution)/shard_map/ppermute | solution.py:48
  7.1 26.3 %collective-permute-start = (f32[256,256]{1,0:T(8,128)S(1)}, f32[256,256]{1,0:T(8,128)S(1)}, u32[]{:S(2)}, u32[]{:S(2)}) collective-permute-start(f32[256,256]{1,0:T(8,128)S(1)} %units.2.refs_0_), channel_id=1, source_target_pairs={{0,4},{4,0},{8,12},{12,8},{16,20},{20,16},{24,28},{28,24},{1,5},{5... | collective-permute-start | bytes 786440 | tf_op jit(solution)/shard_map/ppermute | solution.py:48
  25.6 8.5 %collective-permute-start.2 = (f32[256,256]{1,0:T(8,128)S(1)}, f32[256,256]{1,0:T(8,128)}, u32[]{:S(2)}, u32[]{:S(2)}) collective-permute-start(f32[256,256]{1,0:T(8,128)S(1)} %collective-permute-done.1.refs_2_), channel_id=1, source_target_pairs={{0,4},{4,0},{8,12},{12,8},{16,20},{20,16},{24,28},{28,24},{1,5},{5... | collective-permute-start | bytes 786440 | tf_op jit(solution)/shard_map/ppermute | solution.py:48
  31.9 34.3 %collective-permute-start.23 = (f32[1,10,32,256]{3,2,1,0:T(8,128)}, f32[1,10,32,256]{3,2,1,0:T(8,128)S(1)}, u32[]{:S(2)}, u32[]{:S(2)}) collective-permute-start(f32[1,10,32,256]{3,2,1,0:T(8,128)} %bitcast.6), channel_id=1, source_target_pairs={{0,1},{1,0},{2,3},{3,2},{4,5},{5,4},{6,7},{7,6},{8,9},{9,8},{10,11... | collective-permute-start | bytes 983048 | tf_op jit(solution)/shard_map/ppermute | solution.py:48
  43.2 18.0 %collective-permute-start.3 = (f32[1,4096]{1,0:T(1,128)S(1)}, f32[1,4096]{1,0:T(1,128)S(1)}, u32[]{:S(2)}, u32[]{:S(2)}) collective-permute-start(f32[1,4096]{1,0:T(1,128)S(1)} %get-tuple-element.33.a_ref), channel_id=1, source_target_pairs={{0,8},{4,12},{8,0},{12,4},{16,24},{20,28},{24,16},{28,20},{1,9},{5... | collective-permute-start | bytes 49160 | tf_op jit(solution)/shard_map/ppermute | solution.py:48
  62.6 6.2 %collective-permute-start.4 = (f32[1,6144]{1,0:T(1,128)S(1)}, f32[1,6144]{1,0:T(1,128)S(1)}, u32[]{:S(2)}, u32[]{:S(2)}) collective-permute-start(f32[1,6144]{1,0:T(1,128)S(1)} %row_pass.3), channel_id=1, source_target_pairs={{0,1},{1,0},{2,3},{3,2},{4,5},{5,4},{6,7},{7,6},{8,9},{9,8},{10,11... | collective-permute-start | bytes 73736 | tf_op jit(solution)/shard_map/ppermute | solution.py:48
  63.2 5.6 %collective-permute-start.5 = (f32[1,6144]{1,0:T(1,128)S(1)}, f32[1,6144]{1,0:T(1,128)S(1)}, u32[]{:S(2)}, u32[]{:S(2)}) collective-permute-start(f32[1,6144]{1,0:T(1,128)S(1)} %row_pass.3), channel_id=1, source_target_pairs={{0,2},{1,3},{2,0},{3,1},{4,6},{5,7},{6,4},{7,5},{8,10},{9,11},{10,... | collective-permute-start | bytes 73736 | tf_op jit(solution)/shard_map/ppermute | solution.py:48
  64.8 4.8 %collective-permute-start.6 = (f32[1,6144]{1,0:T(1,128)S(1)}, f32[1,6144]{1,0:T(1,128)S(1)}, u32[]{:S(2)}, u32[]{:S(2)}) collective-permute-start(f32[1,6144]{1,0:T(1,128)S(1)} %row_pass.3), channel_id=1, source_target_pairs={{0,3},{1,2},{2,1},{3,0},{4,7},{5,6},{6,5},{7,4},{8,11},{9,10},{10,... | collective-permute-start | bytes 73736 | tf_op jit(solution)/shard_map/ppermute | solution.py:48
  67.2 15.6 %collective-permute-start.24 = (f32[2,10,32,256]{3,2,1,0:T(8,128)S(1)}, f32[2,10,32,256]{3,2,1,0:T(8,128)S(1)}, u32[]{:S(2)}, u32[]{:S(2)}) collective-permute-start(f32[2,10,32,256]{3,2,1,0:T(8,128)S(1)} %pad_maximum_fusion.1), channel_id=1, source_target_pairs={{0,2},{1,3},{2,0},{3,1},{4,6},{5,7},{6,4},{7,5},{8,10},{9,11},{10,... | collective-permute-start | bytes 1966088 | tf_op jit(solution)/shard_map/ppermute | solution.py:48
  69.6 5.4 %collective-permute-start.7 = (f32[1,6144]{1,0:T(1,128)S(1)}, f32[1,6144]{1,0:T(1,128)S(1)}, u32[]{:S(2)}, u32[]{:S(2)}) collective-permute-start(f32[1,6144]{1,0:T(1,128)S(1)} %add_add_fusion), channel_id=1, source_target_pairs={{0,16},{4,20},{8,24},{12,28},{16,0},{20,4},{24,8},{28,12},{1,17},{... | collective-permute-start | bytes 73736 | tf_op jit(solution)/shard_map/ppermute | solution.py:48
  75.0 1.3 collective-permute-start.8
  75.1 42.7 %collective-permute-start.21 = (f32[1280,256]{1,0:T(8,128)S(1)}, f32[1280,256]{1,0:T(8,128)S(1)}, u32[]{:S(2)}, u32[]{:S(2)}) collective-permute-start(f32[1280,256]{1,0:T(8,128)S(1)} %units.3.unit_ref.own_ref), channel_id=1, source_target_pairs={{0,4},{4,0},{8,12},{12,8},{16,20},{20,16},{24,28},{28,24},{1,5},{5... | collective-permute-start | bytes 3932168 | tf_op jit(solution)/shard_map/ppermute | solution.py:48
  78.2 5.8 %collective-permute-start.9 = (f32[1,4096]{1,0:T(1,128)S(1)}, f32[1,4096]{1,0:T(1,128)S(1)}, u32[]{:S(2)}, u32[]{:S(2)}) collective-permute-start(f32[1,4096]{1,0:T(1,128)S(1)} %column_pass.2.a_ref), channel_id=1, source_target_pairs={{0,8},{4,12},{8,0},{12,4},{16,24},{20,28},{24,16},{28,20},{1,9},{5... | collective-permute-start | bytes 49160 | tf_op jit(solution)/shard_map/ppermute | solution.py:48
  83.9 34.0 %collective-permute-start.25 = (f32[4,10,32,256]{3,2,1,0:T(8,128)S(1)}, f32[4,10,32,256]{3,2,1,0:T(8,128)S(1)}, u32[]{:S(2)}, u32[]{:S(2)}) collective-permute-start(f32[4,10,32,256]{3,2,1,0:T(8,128)S(1)} %pad_maximum_fusion.far_ref), channel_id=1, source_target_pairs={{0,4},{4,0},{8,12},{12,8},{16,20},{20,16},{24,28},{28,24},{1,5},{5... | collective-permute-start | bytes 3932168 | tf_op jit(solution)/shard_map/ppermute | solution.py:48
  85.4 3.7 %collective-permute-start.10 = (f32[1,1024]{1,0:T(1,128)S(1)}, f32[1,1024]{1,0:T(1,128)S(1)}, u32[]{:S(2)}, u32[]{:S(2)}) collective-permute-start(f32[1,1024]{1,0:T(1,128)S(1)} %row_pass.4), channel_id=1, source_target_pairs={{0,1},{1,0},{2,3},{3,2},{4,5},{5,4},{6,7},{7,6},{8,9},{9,8},{10,11... | collective-permute-start | bytes 12296 | tf_op jit(solution)/shard_map/ppermute | solution.py:48
  86.0 3.6 %collective-permute-start.11 = (f32[1,1024]{1,0:T(1,128)S(1)}, f32[1,1024]{1,0:T(1,128)S(1)}, u32[]{:S(2)}, u32[]{:S(2)}) collective-permute-start(f32[1,1024]{1,0:T(1,128)S(1)} %row_pass.4), channel_id=1, source_target_pairs={{0,2},{1,3},{2,0},{3,1},{4,6},{5,7},{6,4},{7,5},{8,10},{9,11},{10,... | collective-permute-start | bytes 12296 | tf_op jit(solution)/shard_map/ppermute | solution.py:48
  87.6 4.5 %collective-permute-start.12 = (f32[1,1024]{1,0:T(1,128)S(1)}, f32[1,1024]{1,0:T(1,128)S(1)}, u32[]{:S(2)}, u32[]{:S(2)}) collective-permute-start(f32[1,1024]{1,0:T(1,128)S(1)} %row_pass.4), channel_id=1, source_target_pairs={{0,3},{1,2},{2,1},{3,0},{4,7},{5,6},{6,5},{7,4},{8,11},{9,10},{10,... | collective-permute-start | bytes 12296 | tf_op jit(solution)/shard_map/ppermute | solution.py:48
  92.1 5.1 %collective-permute-start.13 = (f32[1,1024]{1,0:T(1,128)S(1)}, f32[1,1024]{1,0:T(1,128)S(1)}, u32[]{:S(2)}, u32[]{:S(2)}) collective-permute-start(f32[1,1024]{1,0:T(1,128)S(1)} %add_add_fusion.2), channel_id=1, source_target_pairs={{0,16},{4,20},{8,24},{12,28},{16,0},{20,4},{24,8},{28,12},{1,17},{... | collective-permute-start | bytes 12296 | tf_op jit(solution)/shard_map/ppermute | solution.py:48
  97.2 1.2 collective-permute-start.14
  100.3 3.8 %collective-permute-start.15 = (f32[1,4096]{1,0:T(1,128)S(1)}, f32[1,4096]{1,0:T(1,128)S(1)}, u32[]{:S(2)}, u32[]{:S(2)}) collective-permute-start(f32[1,4096]{1,0:T(1,128)S(1)} %column_pass.3.a_ref), channel_id=1, source_target_pairs={{0,8},{4,12},{8,0},{12,4},{16,24},{20,28},{24,16},{28,20},{1,9},{5... | collective-permute-start | bytes 49160 | tf_op jit(solution)/shard_map/ppermute | solution.py:48
  105.5 3.7 %collective-permute-start.16 = (f32[1,1024]{1,0:T(1,128)S(1)}, f32[1,1024]{1,0:T(1,128)S(1)}, u32[]{:S(2)}, u32[]{:S(2)}) collective-permute-start(f32[1,1024]{1,0:T(1,128)S(1)} %row_pass.5), channel_id=1, source_target_pairs={{0,1},{1,0},{2,3},{3,2},{4,5},{5,4},{6,7},{7,6},{8,9},{9,8},{10,11... | collective-permute-start | bytes 12296 | tf_op jit(solution)/shard_map/ppermute | solution.py:48
  106.8 3.6 %collective-permute-start.17 = (f32[1,1024]{1,0:T(1,128)S(1)}, f32[1,1024]{1,0:T(1,128)S(1)}, u32[]{:S(2)}, u32[]{:S(2)}) collective-permute-start(f32[1,1024]{1,0:T(1,128)S(1)} %row_pass.5), channel_id=1, source_target_pairs={{0,2},{1,3},{2,0},{3,1},{4,6},{5,7},{6,4},{7,5},{8,10},{9,11},{10,... | collective-permute-start | bytes 12296 | tf_op jit(solution)/shard_map/ppermute | solution.py:48
  107.6 4.5 %collective-permute-start.18 = (f32[1,1024]{1,0:T(1,128)S(1)}, f32[1,1024]{1,0:T(1,128)S(1)}, u32[]{:S(2)}, u32[]{:S(2)}) collective-permute-start(f32[1,1024]{1,0:T(1,128)S(1)} %row_pass.5), channel_id=1, source_target_pairs={{0,3},{1,2},{2,1},{3,0},{4,7},{5,6},{6,5},{7,4},{8,11},{9,10},{10,... | collective-permute-start | bytes 12296 | tf_op jit(solution)/shard_map/ppermute | solution.py:48
  112.1 4.6 %collective-permute-start.19 = (f32[1,1024]{1,0:T(1,128)S(1)}, f32[1,1024]{1,0:T(1,128)S(1)}, u32[]{:S(2)}, u32[]{:S(2)}) collective-permute-start(f32[1,1024]{1,0:T(1,128)S(1)} %add_add_fusion.1), channel_id=1, source_target_pairs={{0,16},{4,20},{8,24},{12,28},{16,0},{20,4},{24,8},{28,12},{1,17},{... | collective-permute-start | bytes 12296 | tf_op jit(solution)/shard_map/ppermute | solution.py:48
  116.7 1.2 collective-permute-start.20
  179.0 47.6 %copy-start.14 = (f32[128,512]{1,0:T(8,128)S(1)}, f32[128,512]{1,0:T(8,128)}, u32[]{:S(2)}) copy-start(f32[128,512]{1,0:T(8,128)} %get-tuple-element.53) | copy-start | bytes 786436
  179.0 61.8 %copy-start.15 = (f32[4,10,32,256]{3,2,1,0:T(8,128)S(1)}, f32[4,10,32,256]{3,2,1,0:T(8,128)}, u32[]{:S(2)}) copy-start(f32[4,10,32,256]{3,2,1,0:T(8,128)} %get-tuple-element.48) | copy-start | bytes 3932164
  179.0 62.3 %copy-start.12 = (f32[128,1024]{1,0:T(8,128)S(1)}, f32[128,1024]{1,0:T(8,128)}, u32[]{:S(2)}) copy-start(f32[128,1024]{1,0:T(8,128)} %get-tuple-element.59) | copy-start | bytes 1572868
  179.0 1.4 collective-permute-start.26
  180.4 5.0 %collective-permute-start.27 = (f32[1,128]{1,0:T(1,128)S(1)}, f32[1,128]{1,0:T(1,128)S(1)}, u32[]{:S(2)}, u32[]{:S(2)}) collective-permute-start(f32[1,128]{1,0:T(1,128)S(1)} %add.149), channel_id=1, source_target_pairs={{0,8},{4,12},{8,0},{12,4},{16,24},{20,28},{24,16},{28,20},{1,9},{5... | collective-permute-start | bytes 1544 | tf_op jit(solution)/shard_map/ppermute | solution.py:48
  180.7 4.7 %collective-permute-start.28 = (f32[1,128]{1,0:T(1,128)S(1)}, f32[1,128]{1,0:T(1,128)S(1)}, u32[]{:S(2)}, u32[]{:S(2)}) collective-permute-start(f32[1,128]{1,0:T(1,128)S(1)} %add.149), channel_id=1, source_target_pairs={{0,16},{4,20},{8,24},{12,28},{16,0},{20,4},{24,8},{28,12},{1,17},{... | collective-permute-start | bytes 1544 | tf_op jit(solution)/shard_map/ppermute | solution.py:48
  183.6 5.4 %collective-permute-start.29 = (f32[1,128]{1,0:T(1,128)S(1)}, f32[1,128]{1,0:T(1,128)S(1)}, u32[]{:S(2)}, u32[]{:S(2)}) collective-permute-start(f32[1,128]{1,0:T(1,128)S(1)} %add.149), channel_id=1, source_target_pairs={{0,24},{4,28},{8,16},{12,20},{16,8},{20,12},{24,0},{28,4},{1,25},{... | collective-permute-start | bytes 1544 | tf_op jit(solution)/shard_map/ppermute | solution.py:48
  184.8 11.9 %collective-permute-start.48 = (f32[128,512]{1,0:T(8,128)S(1)}, f32[128,512]{1,0:T(8,128)S(1)}, u32[]{:S(2)}, u32[]{:S(2)}) collective-permute-start(f32[128,512]{1,0:T(8,128)S(1)} %copy-done.19), channel_id=1, source_target_pairs={{0,8},{4,12},{8,0},{12,4},{16,24},{20,28},{24,16},{28,20},{1,9},{5... | collective-permute-start | bytes 786440 | tf_op jit(solution)/shard_map/ppermute | solution.py:48
  189.0 3.6 %collective-permute-start.30 = (f32[1,128]{1,0:T(1,128)S(1)}, f32[1,128]{1,0:T(1,128)S(1)}, u32[]{:S(2)}, u32[]{:S(2)}) collective-permute-start(f32[1,128]{1,0:T(1,128)S(1)} %add_add_fusion.4), channel_id=1, source_target_pairs={{0,1},{1,0},{2,3},{3,2},{4,5},{5,4},{6,7},{7,6},{8,9},{9,8},{10,11... | collective-permute-start | bytes 1544 | tf_op jit(solution)/shard_map/ppermute | solution.py:48
  189.6 5.1 %collective-permute-start.31 = (f32[1,128]{1,0:T(1,128)S(1)}, f32[1,128]{1,0:T(1,128)S(1)}, u32[]{:S(2)}, u32[]{:S(2)}) collective-permute-start(f32[1,128]{1,0:T(1,128)S(1)} %add_add_fusion.4), channel_id=1, source_target_pairs={{0,2},{1,3},{2,0},{3,1},{4,6},{5,7},{6,4},{7,5},{8,10},{9,11},{10,... | collective-permute-start | bytes 1544 | tf_op jit(solution)/shard_map/ppermute | solution.py:48
  191.1 4.5 %collective-permute-start.32 = (f32[1,128]{1,0:T(1,128)S(1)}, f32[1,128]{1,0:T(1,128)S(1)}, u32[]{:S(2)}, u32[]{:S(2)}) collective-permute-start(f32[1,128]{1,0:T(1,128)S(1)} %add_add_fusion.4), channel_id=1, source_target_pairs={{0,3},{1,2},{2,1},{3,0},{4,7},{5,6},{6,5},{7,4},{8,11},{9,10},{10,... | collective-permute-start | bytes 1544 | tf_op jit(solution)/shard_map/ppermute | solution.py:48
  192.5 48.2 %collective-permute-start.56 = (f32[128,1024]{1,0:T(8,128)S(1)}, f32[128,1024]{1,0:T(8,128)S(1)}, u32[]{:S(2)}, u32[]{:S(2)}) collective-permute-start(f32[128,1024]{1,0:T(8,128)S(1)} %copy-done.18), channel_id=1, source_target_pairs={{0,8},{4,12},{8,0},{12,4},{16,24},{20,28},{24,16},{28,20},{1,9},{5... | collective-permute-start | bytes 1572872 | tf_op jit(solution)/shard_map/ppermute | solution.py:48
  192.6 48.8 %collective-permute-start.52 = (f32[128,1024]{1,0:T(8,128)S(1)}, f32[128,1024]{1,0:T(8,128)S(1)}, u32[]{:S(2)}, u32[]{:S(2)}) collective-permute-start(f32[128,1024]{1,0:T(8,128)S(1)} %copy-done.17), channel_id=1, source_target_pairs={{0,8},{4,12},{8,0},{12,4},{16,24},{20,28},{24,16},{28,20},{1,9},{5... | collective-permute-start | bytes 1572872 | tf_op jit(solution)/shard_map/ppermute | solution.py:48
  194.6 31.0 %collective-permute-start.44 = (f32[128,512]{1,0:T(8,128)}, f32[128,512]{1,0:T(8,128)S(1)}, u32[]{:S(2)}, u32[]{:S(2)}) collective-permute-start(f32[128,512]{1,0:T(8,128)} %get-tuple-element.54), channel_id=1, source_target_pairs={{0,8},{4,12},{8,0},{12,4},{16,24},{20,28},{24,16},{28,20},{1,9},{5... | collective-permute-start | bytes 786440 | tf_op jit(solution)/shard_map/ppermute | solution.py:48
  195.5 46.1 %collective-permute-start.40 = (f32[128,1024]{1,0:T(8,128)S(1)}, f32[128,1024]{1,0:T(8,128)S(1)}, u32[]{:S(2)}, u32[]{:S(2)}) collective-permute-start(f32[128,1024]{1,0:T(8,128)S(1)} %copy-done.16), channel_id=1, source_target_pairs={{0,8},{4,12},{8,0},{12,4},{16,24},{20,28},{24,16},{28,20},{1,9},{5... | collective-permute-start | bytes 1572872 | tf_op jit(solution)/shard_map/ppermute | solution.py:48
  196.7 60.2 %collective-permute-start.36 = (f32[4,10,32,256]{3,2,1,0:T(8,128)}, f32[4,10,32,256]{3,2,1,0:T(8,128)S(1)}, u32[]{:S(2)}, u32[]{:S(2)}) collective-permute-start(f32[4,10,32,256]{3,2,1,0:T(8,128)} %get-tuple-element.50), channel_id=1, source_target_pairs={{0,4},{4,0},{8,12},{12,8},{16,20},{20,16},{24,28},{28,24},{1,5},{5... | collective-permute-start | bytes 3932168 | tf_op jit(solution)/shard_map/ppermute | solution.py:48
  196.8 44.7 %copy-start.10 = (f32[128,1024]{1,0:T(8,128)S(1)}, f32[128,1024]{1,0:T(8,128)}, u32[]{:S(2)}) copy-start(f32[128,1024]{1,0:T(8,128)} %get-tuple-element.57) | copy-start | bytes 1572868
  225.6 7.4 %collective-permute-start.50 = (f32[64,512]{1,0:T(8,128)S(1)}, f32[64,512]{1,0:T(8,128)S(1)}, u32[]{:S(2)}, u32[]{:S(2)}) collective-permute-start(f32[64,512]{1,0:T(8,128)S(1)} %slice_add_fusion.10), channel_id=1, source_target_pairs={{0,16},{4,20},{8,24},{12,28},{16,0},{20,4},{24,8},{28,12},{1,17},{... | collective-permute-start | bytes 393224 | tf_op jit(solution)/shard_map/ppermute | solution.py:48
  233.0 7.7 %collective-permute-start.46 = (f32[64,512]{1,0:T(8,128)S(1)}, f32[64,512]{1,0:T(8,128)S(1)}, u32[]{:S(2)}, u32[]{:S(2)}) collective-permute-start(f32[64,512]{1,0:T(8,128)S(1)} %slice_add_fusion.11), channel_id=1, source_target_pairs={{0,16},{4,20},{8,24},{12,28},{16,0},{20,4},{24,8},{28,12},{1,17},{... | collective-permute-start | bytes 393224 | tf_op jit(solution)/shard_map/ppermute | solution.py:48
  240.7 19.5 %collective-permute-start.33 = (f32[4,10,32,256]{3,2,1,0:T(8,128)S(1)}, f32[4,10,32,256]{3,2,1,0:T(8,128)S(1)}, u32[]{:S(2)}, u32[]{:S(2)}) collective-permute-start(f32[4,10,32,256]{3,2,1,0:T(8,128)S(1)} %copy-done.15), channel_id=1, source_target_pairs={{0,4},{4,0},{8,12},{12,8},{16,20},{20,16},{24,28},{28,24},{1,5},{5... | collective-permute-start | bytes 3932168 | tf_op jit(solution)/shard_map/ppermute | solution.py:48
  240.8 41.8 %collective-permute-start.49 = (f32[32,512]{1,0:T(8,128)S(1)}, f32[32,512]{1,0:T(8,128)S(1)}, u32[]{:S(2)}, u32[]{:S(2)}) collective-permute-start(f32[32,512]{1,0:T(8,128)S(1)} %get-tuple-element.69), channel_id=1, source_target_pairs={{0,4},{4,0},{8,12},{12,8},{16,20},{20,16},{24,28},{28,24},{1,5},{5... | collective-permute-start | bytes 196616 | tf_op jit(solution)/shard_map/ppermute | solution.py:48
  241.4 41.7 %collective-permute-start.51 = (f32[32,512]{1,0:T(8,128)S(1)}, f32[32,512]{1,0:T(8,128)S(1)}, u32[]{:S(2)}, u32[]{:S(2)}) collective-permute-start(f32[32,512]{1,0:T(8,128)S(1)} %get-tuple-element.79), channel_id=1, source_target_pairs={{0,4},{4,0},{8,12},{12,8},{16,20},{20,16},{24,28},{28,24},{1,5},{5... | collective-permute-start | bytes 196616 | tf_op jit(solution)/shard_map/ppermute | solution.py:48
  241.6 15.3 %collective-permute-start.58 = (f32[64,1024]{1,0:T(8,128)S(1)}, f32[64,1024]{1,0:T(8,128)S(1)}, u32[]{:S(2)}, u32[]{:S(2)}) collective-permute-start(f32[64,1024]{1,0:T(8,128)S(1)} %slice_add_fusion.3), channel_id=1, source_target_pairs={{0,16},{4,20},{8,24},{12,28},{16,0},{20,4},{24,8},{28,12},{1,17},{... | collective-permute-start | bytes 786440 | tf_op jit(solution)/shard_map/ppermute | solution.py:48
  256.9 20.4 %collective-permute-start.54 = (f32[64,1024]{1,0:T(8,128)S(1)}, f32[64,1024]{1,0:T(8,128)S(1)}, u32[]{:S(2)}, u32[]{:S(2)}) collective-permute-start(f32[64,1024]{1,0:T(8,128)S(1)} %slice_add_fusion.4), channel_id=1, source_target_pairs={{0,16},{4,20},{8,24},{12,28},{16,0},{20,4},{24,8},{28,12},{1,17},{... | collective-permute-start | bytes 786440 | tf_op jit(solution)/shard_map/ppermute | solution.py:48
  256.9 25.6 %collective-permute-start.42 = (f32[64,1024]{1,0:T(8,128)S(1)}, f32[64,1024]{1,0:T(8,128)S(1)}, u32[]{:S(2)}, u32[]{:S(2)}) collective-permute-start(f32[64,1024]{1,0:T(8,128)S(1)} %slice_add_fusion.5), channel_id=1, source_target_pairs={{0,16},{4,20},{8,24},{12,28},{16,0},{20,4},{24,8},{28,12},{1,17},{... | collective-permute-start | bytes 786440 | tf_op jit(solution)/shard_map/ppermute | solution.py:48
  260.3 22.9 %collective-permute-start.37 = (f32[2,1,10,32,256]{4,3,2,1,0:T(8,128)S(1)}, f32[2,1,10,32,256]{4,3,2,1,0:T(8,128)S(1)}, u32[]{:S(2)}, u32[]{:S(2)}) collective-permute-start(f32[2,1,10,32,256]{4,3,2,1,0:T(8,128)S(1)} %slice.209), channel_id=1, source_target_pairs={{0,1},{1,0},{2,3},{3,2},{4,5},{5,4},{6,7},{7,6},{8,9},{9,8},{10,11... | collective-permute-start | bytes 1966088 | tf_op jit(solution)/shard_map/ppermute | solution.py:48
  277.3 17.6 %collective-permute-start.34 = (f32[1,2,10,32,256]{4,3,2,1,0:T(8,128)S(1)}, f32[1,2,10,32,256]{4,3,2,1,0:T(8,128)S(1)}, u32[]{:S(2)}, u32[]{:S(2)}) collective-permute-start(f32[1,2,10,32,256]{4,3,2,1,0:T(8,128)S(1)} %slice_bitcast_fusion), channel_id=1, source_target_pairs={{0,2},{1,3},{2,0},{3,1},{4,6},{5,7},{6,4},{7,5},{8,10},{9,11},{10,... | collective-permute-start | bytes 1966088 | tf_op jit(solution)/shard_map/ppermute | solution.py:48
  282.5 1.3 collective-permute-start.57
  282.5 1.6 collective-permute-start.53
  283.1 1.3 collective-permute-start.59
  283.2 1.4 collective-permute-start.55
  283.8 17.0 %collective-permute-start.45 = (f32[32,512]{1,0:T(8,128)S(1)}, f32[32,512]{1,0:T(8,128)S(1)}, u32[]{:S(2)}, u32[]{:S(2)}) collective-permute-start(f32[32,512]{1,0:T(8,128)S(1)} %get-tuple-element.71), channel_id=1, source_target_pairs={{0,4},{4,0},{8,12},{12,8},{16,20},{20,16},{24,28},{28,24},{1,5},{5... | collective-permute-start | bytes 196616 | tf_op jit(solution)/shard_map/ppermute | solution.py:48
  284.1 16.8 %collective-permute-start.47 = (f32[32,512]{1,0:T(8,128)S(1)}, f32[32,512]{1,0:T(8,128)S(1)}, u32[]{:S(2)}, u32[]{:S(2)}) collective-permute-start(f32[32,512]{1,0:T(8,128)S(1)} %get-tuple-element.81), channel_id=1, source_target_pairs={{0,4},{4,0},{8,12},{12,8},{16,20},{20,16},{24,28},{28,24},{1,5},{5... | collective-permute-start | bytes 196616 | tf_op jit(solution)/shard_map/ppermute | solution.py:48
  284.4 16.5 %collective-permute-start.41 = (f32[32,1024]{1,0:T(8,128)S(1)}, f32[32,1024]{1,0:T(8,128)S(1)}, u32[]{:S(2)}, u32[]{:S(2)}) collective-permute-start(f32[32,1024]{1,0:T(8,128)S(1)} %get-tuple-element.67), channel_id=1, source_target_pairs={{0,4},{4,0},{8,12},{12,8},{16,20},{20,16},{24,28},{28,24},{1,5},{5... | collective-permute-start | bytes 393224 | tf_op jit(solution)/shard_map/ppermute | solution.py:48
  284.6 15.6 %collective-permute-start.38 = (f32[1,1,10,32,256]{4,3,2,1,0:T(8,128)S(1)}, f32[1,1,10,32,256]{4,3,2,1,0:T(8,128)S(1)}, u32[]{:S(2)}, u32[]{:S(2)}) collective-permute-start(f32[1,1,10,32,256]{4,3,2,1,0:T(8,128)S(1)} %slice.211), channel_id=1, source_target_pairs={{0,2},{1,3},{2,0},{3,1},{4,6},{5,7},{6,4},{7,5},{8,10},{9,11},{10,... | collective-permute-start | bytes 983048 | tf_op jit(solution)/shard_map/ppermute | solution.py:48
  294.9 6.1 %collective-permute-start.43 = (f32[32,1024]{1,0:T(8,128)S(1)}, f32[32,1024]{1,0:T(8,128)S(1)}, u32[]{:S(2)}, u32[]{:S(2)}) collective-permute-start(f32[32,1024]{1,0:T(8,128)S(1)} %get-tuple-element.77), channel_id=1, source_target_pairs={{0,4},{4,0},{8,12},{12,8},{16,20},{20,16},{24,28},{28,24},{1,5},{5... | collective-permute-start | bytes 393224 | tf_op jit(solution)/shard_map/ppermute | solution.py:48
  300.2 8.1 %collective-permute-start.35 = (f32[1,1,10,32,256]{4,3,2,1,0:T(8,128)S(1)}, f32[1,1,10,32,256]{4,3,2,1,0:T(8,128)S(1)}, u32[]{:S(2)}, u32[]{:S(2)}) collective-permute-start(f32[1,1,10,32,256]{4,3,2,1,0:T(8,128)S(1)} %slice.207), channel_id=1, source_target_pairs={{0,1},{1,0},{2,3},{3,2},{4,5},{5,4},{6,7},{7,6},{8,9},{9,8},{10,11... | collective-permute-start | bytes 983048 | tf_op jit(solution)/shard_map/ppermute | solution.py:48
  300.8 15.3 %collective-permute-start.39 = (f32[10,32,256]{2,1,0:T(8,128)S(1)}, f32[10,32,256]{2,1,0:T(8,128)S(1)}, u32[]{:S(2)}, u32[]{:S(2)}) collective-permute-start(f32[10,32,256]{2,1,0:T(8,128)S(1)} %fusion.1), channel_id=1, source_target_pairs={{0,16},{4,20},{8,24},{12,28},{16,0},{20,4},{24,8},{28,12},{1,17},{... | collective-permute-start | bytes 983048 | tf_op jit(solution)/shard_map/ppermute | solution.py:48
  (16 other events, 149.6 us)

commit v2 on v1

--- a/solution.py
+++ b/solution.py
@@ -612,7 +612,10 @@
 
     mass, column_sum = teacher_mass(
         places,
-        [teacher_own, teacher_core, teacher_far, teacher_far_core],
+        [
+            pltpu.with_memory_space_constraint(part, pltpu.HBM)
+            for part in (teacher_own, teacher_core, teacher_far, teacher_far_core)
+        ],
         teacher_prototypes,
         columns,
         min(1024, columns),

time: 319 us -> 316 us (level)
  local copies, waits for them, and re-layouts: 6.11 us -> 2.58 us
    unnamed x40 -> x34, local copies, waits for them, and re-layouts: 5.83 us -> 2.3 us
  transfers between devices with their start and end apart: 60 -> 60, of which waited for: 30 -> 30; matrix products, arithmetic and copies ran while one was open for 1% -> 2% of each run, Pallas kernels for 11% -> 12%
where the time goes in v2:
time: 316 us
  waiting for transfers between devices  149 us (47%)
  Pallas kernels  98.5 us (31%)
  starting transfers between devices  58.2 us (18%)
  other arithmetic  4.48 us (1%)
    ppermute x60, waiting for transfers between devices, exchange(): return lax.ppermute(value, axis, [(i, i ^ mask) for i in range(size)])  149 us
    pallas_call x5, Pallas kernels, gradients(): pl.pallas_call(kernel, grid_spec=pltpu.PrefetchScalarGridSpec(num_scalar_...  59.3 us
    ppermute x60, starting transfers between devices, exchange(): return lax.ppermute(value, axis, [(i, i ^ mask) for i in range(size)])  58.2 us
    pallas_call x1, Pallas kernels, row_sums(): pl.pallas_call(kernel, grid=(steps,), in_specs=[SCALARS, pl.BlockSpec((ro...  17.3 us
    pallas_call x1, Pallas kernels, teacher_mass(): pl.pallas_call(kernel, grid_spec=pltpu.PrefetchScalarGridSpec(num_scalar_...  6.41 us
  transfers between devices with their start and end apart: 60, of which 30 were waited for; matrix products, arithmetic and copies ran while one was open for 2% of the time, Pallas kernels for 12%

profile of v2, /device:TPU:0, one launch (start us, length us, event | category | flops | bytes accessed | tf_op | source)
XLA Modules:
  0.0 315.6 jit_solution(5822701811043807740)
XLA Ops:
  1.7 4.1 %collective-permute-start.1 = (f32[256,256]{1,0:T(8,128)S(1)}, f32[256,256]{1,0:T(8,128)S(1)}, u32[]{:S(2)}, u32[]{:S(2)}) collective-permute-start(f32[256,256]{1,0:T(8,128)S(1)} %units.2.refs_0_), channel_id=1, source_target_pairs={{0,16},{4,20},{8,24},{12,28},{16,0},{20,4},{24,8},{28,12},{1,17},{... | collective-permute-start | bytes 786440 | tf_op jit(solution)/shard_map/ppermute | solution.py:48
  6.1 1.0 collective-permute-start.22
  7.2 18.4 %collective-permute-done.1.refs_2_ = f32[256,256]{1,0:T(8,128)S(1)} collective-permute-done((f32[256,256]{1,0:T(8,128)S(1)}, f32[256,256]{1,0:T(8,128)S(1)}, u32[]{:S(2)}, u32[]{:S(2)}) %collective-permute-start.1) | collective-permute-done | bytes 262176 | tf_op jit(solution)/shard_map/ppermute | solution.py:48
  25.7 6.2 %collective-permute-done.22 = f32[10,32,256]{2,1,0:T(8,128)} collective-permute-done((f32[10,32,256]{2,1,0:T(8,128)S(1)}, f32[10,32,256]{2,1,0:T(8,128)}, u32[]{:S(2)}, u32[]{:S(2)}) %collective-permute-start.22) | collective-permute-done | bytes 327712 | tf_op jit(solution)/shard_map/ppermute | solution.py:48
  31.9 1.5 collective-permute-start.23
  34.1 6.4 %teacher_mass.1 = (f32[1024,4096]{1,0:T(8,128)S(1)}, f32[1,4096]{1,0:T(1,128)S(1)}) custom-call(s32[3]{0:T(128)S(1)} %pad_add_fusion.2.place_ref, f32[256,256]{1,0:T(8,128)} %copy-done.1, f32[256,256]{1,0:T(8,128)} %copy-done.16, f32[256,256]{1,0:T(8,128)} %copy-done.15, f32[256,256]{1,0:T(8,128)} %collective-permute-done.2.refs_3_, bf16[256,16384]{1,0:T(8,128)(2,1)} %refs_4_.1), custom_call_target="tpu_custom_call" | custom-call | flops 5000000000 | bytes 5000000 | tf_op jit(solution)/shard_map/teacher_mass/pallas_call | solution.py:184
  41.2 17.3 %row_sums.1.refs_0_ = f32[1,5120]{1,0:T(1,128)S(1)} custom-call(s32[3]{0:T(128)S(1)} %pad_add_fusion.2.place_ref, f32[1280,256]{1,0:T(8,128)S(1)} %units.3.unit_ref.own_ref, bf16[256,16384]{1,0:T(8,128)(2,1)} %refs_0_.9), custom_call_target="tpu_custom_call" | custom-call | flops 15000000512 | bytes 15000000 | tf_op jit(solution)/shard_map/row_sums/pallas_call | solution.py:135
  58.5 1.5 row_pass.3
  60.6 1.5 collective-permute-start.5
  62.1 1.4 collective-permute-start.6
  63.5 1.0 pad_maximum_fusion.1
  64.6 1.6 collective-permute-start.24
  67.0 3.5 %collective-permute-start.7 = (f32[1,6144]{1,0:T(1,128)S(1)}, f32[1,6144]{1,0:T(1,128)S(1)}, u32[]{:S(2)}, u32[]{:S(2)}) collective-permute-start(f32[1,6144]{1,0:T(1,128)S(1)} %add_add_fusion), channel_id=1, source_target_pairs={{0,16},{4,20},{8,24},{12,28},{16,0},{20,4},{24,8},{28,12},{1,17},{... | collective-permute-start | bytes 73736 | tf_op jit(solution)/shard_map/ppermute | solution.py:48
  70.5 1.8 collective-permute-done.7
  73.6 1.9 column_pass.2.a_ref
  76.5 3.7 %collective-permute-done.24 = f32[2,10,32,256]{3,2,1,0:T(8,128)S(1)} collective-permute-done((f32[2,10,32,256]{3,2,1,0:T(8,128)S(1)}, f32[2,10,32,256]{3,2,1,0:T(8,128)S(1)}, u32[]{:S(2)}, u32[]{:S(2)}) %collective-permute-start.24) | collective-permute-done | bytes 655392 | tf_op jit(solution)/shard_map/ppermute | solution.py:48
  80.2 1.1 pad_maximum_fusion.far_ref
  81.3 1.5 row_pass.4
  83.4 1.5 collective-permute-start.11
  84.9 1.4 collective-permute-start.12
  87.0 2.4 collective-permute-done.12
  89.4 3.5 %collective-permute-start.13 = (f32[1,1024]{1,0:T(1,128)S(1)}, f32[1,1024]{1,0:T(1,128)S(1)}, u32[]{:S(2)}, u32[]{:S(2)}) collective-permute-start(f32[1,1024]{1,0:T(1,128)S(1)} %add_add_fusion.2), channel_id=1, source_target_pairs={{0,16},{4,20},{8,24},{12,28},{16,0},{20,4},{24,8},{28,12},{1,17},{... | collective-permute-start | bytes 12296 | tf_op jit(solution)/shard_map/ppermute | solution.py:48
  93.0 1.6 collective-permute-done.13
  94.6 1.2 collective-permute-done.14.b_ref
  95.7 1.9 column_pass.3.a_ref
  98.0 3.4 %collective-permute-done.15.b_ref = f32[1,4096]{1,0:T(1,128)S(1)} collective-permute-done((f32[1,4096]{1,0:T(1,128)S(1)}, f32[1,4096]{1,0:T(1,128)S(1)}, u32[]{:S(2)}, u32[]{:S(2)}) %collective-permute-start.15) | collective-permute-done | bytes 16416 | tf_op jit(solution)/shard_map/ppermute | solution.py:48
  101.4 1.5 row_pass.5
  102.9 1.3 collective-permute-start.16
  104.9 1.5 collective-permute-start.18
  106.5 1.2 collective-permute-done.17
  107.8 1.7 collective-permute-done.18
  109.5 3.0 collective-permute-start.19
  112.5 1.5 collective-permute-done.19
  114.0 1.1 row_offsets.1
  115.2 1.8 gather_rows.1
  117.0 8.5 %gradients.5 = (f32[128,512]{1,0:T(8,128)}, f32[128,512]{1,0:T(8,128)}, f32[4,10,128,256]{3,2,1,0:T(8,128)S(1)}, f32[1024,256]{1,0:T(8,128)S(1)}) custom-call(s32[4]{0:T(128)S(1)} %get-tuple-element.61.place_ref, bf16[256,16384]{1,0:T(8,128)(2,1)} %refs_0_.9, f32[1024,4096]{1,0:T(8,128)S(1)} %get-tuple-element.32.mass_ref.refs_1_, ...), custom_call_target="tpu_custom_call" | custom-call | flops 10000000000 | bytes 10000000 | tf_op jit(solution)/shard_map/gradients/pallas_call | solution.py:505
  125.5 14.0 %gradients.6 = (f32[128,1024]{1,0:T(8,128)}, f32[128,1024]{1,0:T(8,128)}, f32[4,10,128,256]{3,2,1,0:T(8,128)S(1)}, f32[1024,256]{1,0:T(8,128)S(1)}) custom-call(s32[4]{0:T(128)S(1)} %get-tuple-element.83.place_ref, bf16[256,16384]{1,0:T(8,128)(2,1)} %refs_0_.9, ...), custom_call_target="tpu_custom_call", output_to_operand_aliasing={{2}: (8, {}), {3}: (9, {})} | custom-call | flops 10000000000 | bytes 10000000 | tf_op jit(solution)/shard_map/gradients/pallas_call | solution.py:505
  139.5 13.8 %gradients.7 = (f32[128,1024]{1,0:T(8,128)}, f32[128,1024]{1,0:T(8,128)}, f32[4,10,128,256]{3,2,1,0:T(8,128)S(1)}, f32[1024,256]{1,0:T(8,128)S(1)}) custom-call(s32[4]{0:T(128)S(1)} %get-tuple-element.84.place_ref, bf16[256,16384]{1,0:T(8,128)(2,1)} %refs_0_.9, ...), custom_call_target="tpu_custom_call", output_to_operand_aliasing={{2}: (8, {}), {3}: (9, {})} | custom-call | flops 10000000000 | bytes 10000000 | tf_op jit(solution)/shard_map/gradients/pallas_call | solution.py:505
  153.2 14.0 %gradients.8 = (f32[128,1024]{1,0:T(8,128)}, f32[128,1024]{1,0:T(8,128)}, f32[4,10,128,256]{3,2,1,0:T(8,128)S(1)}, f32[1024,256]{1,0:T(8,128)S(1)}) custom-call(s32[4]{0:T(128)S(1)} %get-tuple-element.85.place_ref, bf16[256,16384]{1,0:T(8,128)(2,1)} %refs_0_.9, ...), custom_call_target="tpu_custom_call", output_to_operand_aliasing={{2}: (8, {}), {3}: (9, {})} | custom-call | flops 10000000000 | bytes 10000000 | tf_op jit(solution)/shard_map/gradients/pallas_call | solution.py:505
  167.3 9.1 %gradients.9 = (f32[128,512]{1,0:T(8,128)}, f32[128,512]{1,0:T(8,128)}, f32[4,10,32,256]{3,2,1,0:T(8,128)}, f32[4,10,32,256]{3,2,1,0:T(8,128)}, f32[4,10,32,256]...) custom-call(s32[4]{0:T(128)S(1)} %get-tuple-element.86.place_ref, bf16[256,16384]{1,0:T(8,128)(2,1)} %refs_0_.9, ...), custom_call_target="tpu_custom_call" | custom-call | flops 10000000000 | bytes 10000000 | tf_op jit(solution)/shard_map/gradients/pallas_call | solution.py:505
  178.1 2.9 collective-permute-start.28
  181.0 1.1 collective-permute-start.29
  182.8 3.6 %collective-permute-done.29 = f32[1,128]{1,0:T(1,128)S(1)} collective-permute-done((f32[1,128]{1,0:T(1,128)S(1)}, f32[1,128]{1,0:T(1,128)S(1)}, u32[]{:S(2)}, u32[]{:S(2)}) %collective-permute-start.29) | collective-permute-done | bytes 544 | tf_op jit(solution)/shard_map/ppermute | solution.py:48
  187.0 1.5 collective-permute-start.31
  188.5 1.4 collective-permute-start.32
  190.0 2.0 collective-permute-start.52
  192.9 1.1 collective-permute-start.40
  194.3 28.8 %collective-permute-done.44 = f32[128,512]{1,0:T(8,128)S(1)} collective-permute-done((f32[128,512]{1,0:T(8,128)}, f32[128,512]{1,0:T(8,128)S(1)}, u32[]{:S(2)}, u32[]{:S(2)}) %collective-permute-start.44) | collective-permute-done | bytes 262176 | tf_op jit(solution)/shard_map/ppermute | solution.py:48
  224.0 6.4 %collective-permute-done.50 = f32[64,512]{1,0:T(8,128)S(1)} collective-permute-done((f32[64,512]{1,0:T(8,128)S(1)}, f32[64,512]{1,0:T(8,128)S(1)}, u32[]{:S(2)}, u32[]{:S(2)}) %collective-permute-start.50) | collective-permute-done | bytes 131104 | tf_op jit(solution)/shard_map/ppermute | solution.py:48
  230.4 3.4 %collective-permute-start.46 = (f32[64,512]{1,0:T(8,128)S(1)}, f32[64,512]{1,0:T(8,128)S(1)}, u32[]{:S(2)}, u32[]{:S(2)}) collective-permute-start(f32[64,512]{1,0:T(8,128)S(1)} %slice_add_fusion.11), channel_id=1, source_target_pairs={{0,16},{4,20},{8,24},{12,28},{16,0},{20,4},{24,8},{28,12},{1,17},{... | collective-permute-start | bytes 393224 | tf_op jit(solution)/shard_map/ppermute | solution.py:48
  233.8 4.3 %collective-permute-done.46 = f32[64,512]{1,0:T(8,128)S(1)} collective-permute-done((f32[64,512]{1,0:T(8,128)S(1)}, f32[64,512]{1,0:T(8,128)S(1)}, u32[]{:S(2)}, u32[]{:S(2)}) %collective-permute-start.46) | collective-permute-done | bytes 131104 | tf_op jit(solution)/shard_map/ppermute | solution.py:48
  239.0 1.7 collective-permute-start.58
  240.8 13.5 %collective-permute-done.58 = f32[64,1024]{1,0:T(8,128)S(1)} collective-permute-done((f32[64,1024]{1,0:T(8,128)S(1)}, f32[64,1024]{1,0:T(8,128)S(1)}, u32[]{:S(2)}, u32[]{:S(2)}) %collective-permute-start.58) | collective-permute-done | bytes 262176 | tf_op jit(solution)/shard_map/ppermute | solution.py:48
  254.4 3.0 collective-permute-start.42
  259.2 15.5 %collective-permute-done.54 = f32[64,1024]{1,0:T(8,128)S(1)} collective-permute-done((f32[64,1024]{1,0:T(8,128)S(1)}, f32[64,1024]{1,0:T(8,128)S(1)}, u32[]{:S(2)}, u32[]{:S(2)}) %collective-permute-start.54) | collective-permute-done | bytes 262176 | tf_op jit(solution)/shard_map/ppermute | solution.py:48
  274.7 1.2 collective-permute-start.34
  276.0 3.9 %collective-permute-done.42 = f32[64,1024]{1,0:T(8,128)S(1)} collective-permute-done((f32[64,1024]{1,0:T(8,128)S(1)}, f32[64,1024]{1,0:T(8,128)S(1)}, u32[]{:S(2)}, u32[]{:S(2)}) %collective-permute-start.42) | collective-permute-done | bytes 262176 | tf_op jit(solution)/shard_map/ppermute | solution.py:48
  282.1 1.2 collective-permute-start.38
  283.3 1.7 assemble.2.refs_8_
  285.0 7.3 %collective-permute-done.34 = f32[1,2,10,32,256]{4,3,2,1,0:T(8,128)S(1)} collective-permute-done((f32[1,2,10,32,256]{4,3,2,1,0:T(8,128)S(1)}, f32[1,2,10,32,256]{4,3,2,1,0:T(8,128)S(1)}, u32[]{:S(2)}, u32[]{:S(2)}) %collective-permute-start.34) | collective-permute-done | bytes 655392 | tf_op jit(solution)/shard_map/ppermute | solution.py:48
  292.4 5.2 %collective-permute-done.38 = f32[1,1,10,32,256]{4,3,2,1,0:T(8,128)S(1)} collective-permute-done((f32[1,1,10,32,256]{4,3,2,1,0:T(8,128)S(1)}, f32[1,1,10,32,256]{4,3,2,1,0:T(8,128)S(1)}, u32[]{:S(2)}, u32[]{:S(2)}) %collective-permute-start.38) | collective-permute-done | bytes 327712 | tf_op jit(solution)/shard_map/ppermute | solution.py:48
  298.4 1.5 assemble.3
  299.8 5.9 %collective-permute-done.35 = f32[1,1,10,32,256]{4,3,2,1,0:T(8,128)S(1)} collective-permute-done((f32[1,1,10,32,256]{4,3,2,1,0:T(8,128)S(1)}, f32[1,1,10,32,256]{4,3,2,1,0:T(8,128)S(1)}, u32[]{:S(2)}, u32[]{:S(2)}) %collective-permute-start.35) | collective-permute-done | bytes 327712 | tf_op jit(solution)/shard_map/ppermute | solution.py:48
  305.8 7.8 %collective-permute-done.39 = f32[10,32,256]{2,1,0:T(8,128)S(1)} collective-permute-done((f32[10,32,256]{2,1,0:T(8,128)S(1)}, f32[10,32,256]{2,1,0:T(8,128)S(1)}, u32[]{:S(2)}, u32[]{:S(2)}) %collective-permute-start.39) | collective-permute-done | bytes 327712 | tf_op jit(solution)/shard_map/ppermute | solution.py:48
  (153 shorter events, 20.7 us)
Async XLA Ops:
  1.7 23.9 %collective-permute-start.1 = (f32[256,256]{1,0:T(8,128)S(1)}, f32[256,256]{1,0:T(8,128)S(1)}, u32[]{:S(2)}, u32[]{:S(2)}) collective-permute-start(f32[256,256]{1,0:T(8,128)S(1)} %units.2.refs_0_), channel_id=1, source_target_pairs={{0,16},{4,20},{8,24},{12,28},{16,0},{20,4},{24,8},{28,12},{1,17},{... | collective-permute-start | bytes 786440 | tf_op jit(solution)/shard_map/ppermute | solution.py:48
  6.1 25.8 %collective-permute-start.22 = (f32[10,32,256]{2,1,0:T(8,128)S(1)}, f32[10,32,256]{2,1,0:T(8,128)}, u32[]{:S(2)}, u32[]{:S(2)}) collective-permute-start(f32[10,32,256]{2,1,0:T(8,128)S(1)} %constant_dynamic-slice_fusion.1), channel_id=1, source_target_pairs={{0,16},{4,20},{8,24},{12,28},{16,0},{20,4},{24,8},{28,12},{1,17},{... | collective-permute-start | bytes 983048 | tf_op jit(solution)/shard_map/ppermute | solution.py:48
  7.1 26.3 %collective-permute-start = (f32[256,256]{1,0:T(8,128)S(1)}, f32[256,256]{1,0:T(8,128)S(1)}, u32[]{:S(2)}, u32[]{:S(2)}) collective-permute-start(f32[256,256]{1,0:T(8,128)S(1)} %units.2.refs_0_), channel_id=1, source_target_pairs={{0,4},{4,0},{8,12},{12,8},{16,20},{20,16},{24,28},{28,24},{1,5},{5... | collective-permute-start | bytes 786440 | tf_op jit(solution)/shard_map/ppermute | solution.py:48
  25.6 8.5 %collective-permute-start.2 = (f32[256,256]{1,0:T(8,128)S(1)}, f32[256,256]{1,0:T(8,128)}, u32[]{:S(2)}, u32[]{:S(2)}) collective-permute-start(f32[256,256]{1,0:T(8,128)S(1)} %collective-permute-done.1.refs_2_), channel_id=1, source_target_pairs={{0,4},{4,0},{8,12},{12,8},{16,20},{20,16},{24,28},{28,24},{1,5},{5... | collective-permute-start | bytes 786440 | tf_op jit(solution)/shard_map/ppermute | solution.py:48
  31.9 31.7 %collective-permute-start.23 = (f32[1,10,32,256]{3,2,1,0:T(8,128)}, f32[1,10,32,256]{3,2,1,0:T(8,128)S(1)}, u32[]{:S(2)}, u32[]{:S(2)}) collective-permute-start(f32[1,10,32,256]{3,2,1,0:T(8,128)} %bitcast.6), channel_id=1, source_target_pairs={{0,1},{1,0},{2,3},{3,2},{4,5},{5,4},{6,7},{7,6},{8,9},{9,8},{10,11... | collective-permute-start | bytes 983048 | tf_op jit(solution)/shard_map/ppermute | solution.py:48
  40.5 18.0 %collective-permute-start.3 = (f32[1,4096]{1,0:T(1,128)S(1)}, f32[1,4096]{1,0:T(1,128)S(1)}, u32[]{:S(2)}, u32[]{:S(2)}) collective-permute-start(f32[1,4096]{1,0:T(1,128)S(1)} %get-tuple-element.33.a_ref), channel_id=1, source_target_pairs={{0,8},{4,12},{8,0},{12,4},{16,24},{20,28},{24,16},{28,20},{1,9},{5... | collective-permute-start | bytes 49160 | tf_op jit(solution)/shard_map/ppermute | solution.py:48
  60.0 6.2 %collective-permute-start.4 = (f32[1,6144]{1,0:T(1,128)S(1)}, f32[1,6144]{1,0:T(1,128)S(1)}, u32[]{:S(2)}, u32[]{:S(2)}) collective-permute-start(f32[1,6144]{1,0:T(1,128)S(1)} %row_pass.3), channel_id=1, source_target_pairs={{0,1},{1,0},{2,3},{3,2},{4,5},{5,4},{6,7},{7,6},{8,9},{9,8},{10,11... | collective-permute-start | bytes 73736 | tf_op jit(solution)/shard_map/ppermute | solution.py:48
  60.6 5.6 %collective-permute-start.5 = (f32[1,6144]{1,0:T(1,128)S(1)}, f32[1,6144]{1,0:T(1,128)S(1)}, u32[]{:S(2)}, u32[]{:S(2)}) collective-permute-start(f32[1,6144]{1,0:T(1,128)S(1)} %row_pass.3), channel_id=1, source_target_pairs={{0,2},{1,3},{2,0},{3,1},{4,6},{5,7},{6,4},{7,5},{8,10},{9,11},{10,... | collective-permute-start | bytes 73736 | tf_op jit(solution)/shard_map/ppermute | solution.py:48
  62.1 4.8 %collective-permute-start.6 = (f32[1,6144]{1,0:T(1,128)S(1)}, f32[1,6144]{1,0:T(1,128)S(1)}, u32[]{:S(2)}, u32[]{:S(2)}) collective-permute-start(f32[1,6144]{1,0:T(1,128)S(1)} %row_pass.3), channel_id=1, source_target_pairs={{0,3},{1,2},{2,1},{3,0},{4,7},{5,6},{6,5},{7,4},{8,11},{9,10},{10,... | collective-permute-start | bytes 73736 | tf_op jit(solution)/shard_map/ppermute | solution.py:48
  64.6 15.6 %collective-permute-start.24 = (f32[2,10,32,256]{3,2,1,0:T(8,128)S(1)}, f32[2,10,32,256]{3,2,1,0:T(8,128)S(1)}, u32[]{:S(2)}, u32[]{:S(2)}) collective-permute-start(f32[2,10,32,256]{3,2,1,0:T(8,128)S(1)} %pad_maximum_fusion.1), channel_id=1, source_target_pairs={{0,2},{1,3},{2,0},{3,1},{4,6},{5,7},{6,4},{7,5},{8,10},{9,11},{10,... | collective-permute-start | bytes 1966088 | tf_op jit(solution)/shard_map/ppermute | solution.py:48
  67.0 5.4 %collective-permute-start.7 = (f32[1,6144]{1,0:T(1,128)S(1)}, f32[1,6144]{1,0:T(1,128)S(1)}, u32[]{:S(2)}, u32[]{:S(2)}) collective-permute-start(f32[1,6144]{1,0:T(1,128)S(1)} %add_add_fusion), channel_id=1, source_target_pairs={{0,16},{4,20},{8,24},{12,28},{16,0},{20,4},{24,8},{28,12},{1,17},{... | collective-permute-start | bytes 73736 | tf_op jit(solution)/shard_map/ppermute | solution.py:48
  72.4 1.3 collective-permute-start.8
  72.4 42.8 %collective-permute-start.21 = (f32[1280,256]{1,0:T(8,128)S(1)}, f32[1280,256]{1,0:T(8,128)S(1)}, u32[]{:S(2)}, u32[]{:S(2)}) collective-permute-start(f32[1280,256]{1,0:T(8,128)S(1)} %units.3.unit_ref.own_ref), channel_id=1, source_target_pairs={{0,4},{4,0},{8,12},{12,8},{16,20},{20,16},{24,28},{28,24},{1,5},{5... | collective-permute-start | bytes 3932168 | tf_op jit(solution)/shard_map/ppermute | solution.py:48
  75.5 5.8 %collective-permute-start.9 = (f32[1,4096]{1,0:T(1,128)S(1)}, f32[1,4096]{1,0:T(1,128)S(1)}, u32[]{:S(2)}, u32[]{:S(2)}) collective-permute-start(f32[1,4096]{1,0:T(1,128)S(1)} %column_pass.2.a_ref), channel_id=1, source_target_pairs={{0,8},{4,12},{8,0},{12,4},{16,24},{20,28},{24,16},{28,20},{1,9},{5... | collective-permute-start | bytes 49160 | tf_op jit(solution)/shard_map/ppermute | solution.py:48
  81.2 34.0 %collective-permute-start.25 = (f32[4,10,32,256]{3,2,1,0:T(8,128)S(1)}, f32[4,10,32,256]{3,2,1,0:T(8,128)S(1)}, u32[]{:S(2)}, u32[]{:S(2)}) collective-permute-start(f32[4,10,32,256]{3,2,1,0:T(8,128)S(1)} %pad_maximum_fusion.far_ref), channel_id=1, source_target_pairs={{0,4},{4,0},{8,12},{12,8},{16,20},{20,16},{24,28},{28,24},{1,5},{5... | collective-permute-start | bytes 3932168 | tf_op jit(solution)/shard_map/ppermute | solution.py:48
  82.8 3.7 %collective-permute-start.10 = (f32[1,1024]{1,0:T(1,128)S(1)}, f32[1,1024]{1,0:T(1,128)S(1)}, u32[]{:S(2)}, u32[]{:S(2)}) collective-permute-start(f32[1,1024]{1,0:T(1,128)S(1)} %row_pass.4), channel_id=1, source_target_pairs={{0,1},{1,0},{2,3},{3,2},{4,5},{5,4},{6,7},{7,6},{8,9},{9,8},{10,11... | collective-permute-start | bytes 12296 | tf_op jit(solution)/shard_map/ppermute | solution.py:48
  83.4 3.6 %collective-permute-start.11 = (f32[1,1024]{1,0:T(1,128)S(1)}, f32[1,1024]{1,0:T(1,128)S(1)}, u32[]{:S(2)}, u32[]{:S(2)}) collective-permute-start(f32[1,1024]{1,0:T(1,128)S(1)} %row_pass.4), channel_id=1, source_target_pairs={{0,2},{1,3},{2,0},{3,1},{4,6},{5,7},{6,4},{7,5},{8,10},{9,11},{10,... | collective-permute-start | bytes 12296 | tf_op jit(solution)/shard_map/ppermute | solution.py:48
  84.9 4.5 %collective-permute-start.12 = (f32[1,1024]{1,0:T(1,128)S(1)}, f32[1,1024]{1,0:T(1,128)S(1)}, u32[]{:S(2)}, u32[]{:S(2)}) collective-permute-start(f32[1,1024]{1,0:T(1,128)S(1)} %row_pass.4), channel_id=1, source_target_pairs={{0,3},{1,2},{2,1},{3,0},{4,7},{5,6},{6,5},{7,4},{8,11},{9,10},{10,... | collective-permute-start | bytes 12296 | tf_op jit(solution)/shard_map/ppermute | solution.py:48
  89.4 5.1 %collective-permute-start.13 = (f32[1,1024]{1,0:T(1,128)S(1)}, f32[1,1024]{1,0:T(1,128)S(1)}, u32[]{:S(2)}, u32[]{:S(2)}) collective-permute-start(f32[1,1024]{1,0:T(1,128)S(1)} %add_add_fusion.2), channel_id=1, source_target_pairs={{0,16},{4,20},{8,24},{12,28},{16,0},{20,4},{24,8},{28,12},{1,17},{... | collective-permute-start | bytes 12296 | tf_op jit(solution)/shard_map/ppermute | solution.py:48
  94.6 1.2 collective-permute-start.14
  97.6 3.8 %collective-permute-start.15 = (f32[1,4096]{1,0:T(1,128)S(1)}, f32[1,4096]{1,0:T(1,128)S(1)}, u32[]{:S(2)}, u32[]{:S(2)}) collective-permute-start(f32[1,4096]{1,0:T(1,128)S(1)} %column_pass.3.a_ref), channel_id=1, source_target_pairs={{0,8},{4,12},{8,0},{12,4},{16,24},{20,28},{24,16},{28,20},{1,9},{5... | collective-permute-start | bytes 49160 | tf_op jit(solution)/shard_map/ppermute | solution.py:48
  102.9 3.7 %collective-permute-start.16 = (f32[1,1024]{1,0:T(1,128)S(1)}, f32[1,1024]{1,0:T(1,128)S(1)}, u32[]{:S(2)}, u32[]{:S(2)}) collective-permute-start(f32[1,1024]{1,0:T(1,128)S(1)} %row_pass.5), channel_id=1, source_target_pairs={{0,1},{1,0},{2,3},{3,2},{4,5},{5,4},{6,7},{7,6},{8,9},{9,8},{10,11... | collective-permute-start | bytes 12296 | tf_op jit(solution)/shard_map/ppermute | solution.py:48
  104.2 3.6 %collective-permute-start.17 = (f32[1,1024]{1,0:T(1,128)S(1)}, f32[1,1024]{1,0:T(1,128)S(1)}, u32[]{:S(2)}, u32[]{:S(2)}) collective-permute-start(f32[1,1024]{1,0:T(1,128)S(1)} %row_pass.5), channel_id=1, source_target_pairs={{0,2},{1,3},{2,0},{3,1},{4,6},{5,7},{6,4},{7,5},{8,10},{9,11},{10,... | collective-permute-start | bytes 12296 | tf_op jit(solution)/shard_map/ppermute | solution.py:48
  104.9 4.5 %collective-permute-start.18 = (f32[1,1024]{1,0:T(1,128)S(1)}, f32[1,1024]{1,0:T(1,128)S(1)}, u32[]{:S(2)}, u32[]{:S(2)}) collective-permute-start(f32[1,1024]{1,0:T(1,128)S(1)} %row_pass.5), channel_id=1, source_target_pairs={{0,3},{1,2},{2,1},{3,0},{4,7},{5,6},{6,5},{7,4},{8,11},{9,10},{10,... | collective-permute-start | bytes 12296 | tf_op jit(solution)/shard_map/ppermute | solution.py:48
  109.5 4.6 %collective-permute-start.19 = (f32[1,1024]{1,0:T(1,128)S(1)}, f32[1,1024]{1,0:T(1,128)S(1)}, u32[]{:S(2)}, u32[]{:S(2)}) collective-permute-start(f32[1,1024]{1,0:T(1,128)S(1)} %add_add_fusion.1), channel_id=1, source_target_pairs={{0,16},{4,20},{8,24},{12,28},{16,0},{20,4},{24,8},{28,12},{1,17},{... | collective-permute-start | bytes 12296 | tf_op jit(solution)/shard_map/ppermute | solution.py:48
  114.0 1.2 collective-permute-start.20
  176.4 47.6 %copy-start.9 = (f32[128,512]{1,0:T(8,128)S(1)}, f32[128,512]{1,0:T(8,128)}, u32[]{:S(2)}) copy-start(f32[128,512]{1,0:T(8,128)} %get-tuple-element.53) | copy-start | bytes 786436
  176.4 61.8 %copy-start.10 = (f32[4,10,32,256]{3,2,1,0:T(8,128)S(1)}, f32[4,10,32,256]{3,2,1,0:T(8,128)}, u32[]{:S(2)}) copy-start(f32[4,10,32,256]{3,2,1,0:T(8,128)} %get-tuple-element.48) | copy-start | bytes 3932164
  176.4 62.3 %copy-start.7 = (f32[128,1024]{1,0:T(8,128)S(1)}, f32[128,1024]{1,0:T(8,128)}, u32[]{:S(2)}) copy-start(f32[128,1024]{1,0:T(8,128)} %get-tuple-element.59) | copy-start | bytes 1572868
  176.4 1.4 collective-permute-start.26
  177.8 5.0 %collective-permute-start.27 = (f32[1,128]{1,0:T(1,128)S(1)}, f32[1,128]{1,0:T(1,128)S(1)}, u32[]{:S(2)}, u32[]{:S(2)}) collective-permute-start(f32[1,128]{1,0:T(1,128)S(1)} %add.149), channel_id=1, source_target_pairs={{0,8},{4,12},{8,0},{12,4},{16,24},{20,28},{24,16},{28,20},{1,9},{5... | collective-permute-start | bytes 1544 | tf_op jit(solution)/shard_map/ppermute | solution.py:48
  178.1 4.7 %collective-permute-start.28 = (f32[1,128]{1,0:T(1,128)S(1)}, f32[1,128]{1,0:T(1,128)S(1)}, u32[]{:S(2)}, u32[]{:S(2)}) collective-permute-start(f32[1,128]{1,0:T(1,128)S(1)} %add.149), channel_id=1, source_target_pairs={{0,16},{4,20},{8,24},{12,28},{16,0},{20,4},{24,8},{28,12},{1,17},{... | collective-permute-start | bytes 1544 | tf_op jit(solution)/shard_map/ppermute | solution.py:48
  181.0 5.4 %collective-permute-start.29 = (f32[1,128]{1,0:T(1,128)S(1)}, f32[1,128]{1,0:T(1,128)S(1)}, u32[]{:S(2)}, u32[]{:S(2)}) collective-permute-start(f32[1,128]{1,0:T(1,128)S(1)} %add.149), channel_id=1, source_target_pairs={{0,24},{4,28},{8,16},{12,20},{16,8},{20,12},{24,0},{28,4},{1,25},{... | collective-permute-start | bytes 1544 | tf_op jit(solution)/shard_map/ppermute | solution.py:48
  182.2 11.9 %collective-permute-start.48 = (f32[128,512]{1,0:T(8,128)S(1)}, f32[128,512]{1,0:T(8,128)S(1)}, u32[]{:S(2)}, u32[]{:S(2)}) collective-permute-start(f32[128,512]{1,0:T(8,128)S(1)} %copy-done.14), channel_id=1, source_target_pairs={{0,8},{4,12},{8,0},{12,4},{16,24},{20,28},{24,16},{28,20},{1,9},{5... | collective-permute-start | bytes 786440 | tf_op jit(solution)/shard_map/ppermute | solution.py:48
  186.4 3.6 %collective-permute-start.30 = (f32[1,128]{1,0:T(1,128)S(1)}, f32[1,128]{1,0:T(1,128)S(1)}, u32[]{:S(2)}, u32[]{:S(2)}) collective-permute-start(f32[1,128]{1,0:T(1,128)S(1)} %add_add_fusion.4), channel_id=1, source_target_pairs={{0,1},{1,0},{2,3},{3,2},{4,5},{5,4},{6,7},{7,6},{8,9},{9,8},{10,11... | collective-permute-start | bytes 1544 | tf_op jit(solution)/shard_map/ppermute | solution.py:48
  187.0 5.1 %collective-permute-start.31 = (f32[1,128]{1,0:T(1,128)S(1)}, f32[1,128]{1,0:T(1,128)S(1)}, u32[]{:S(2)}, u32[]{:S(2)}) collective-permute-start(f32[1,128]{1,0:T(1,128)S(1)} %add_add_fusion.4), channel_id=1, source_target_pairs={{0,2},{1,3},{2,0},{3,1},{4,6},{5,7},{6,4},{7,5},{8,10},{9,11},{10,... | collective-permute-start | bytes 1544 | tf_op jit(solution)/shard_map/ppermute | solution.py:48
  188.5 4.5 %collective-permute-start.32 = (f32[1,128]{1,0:T(1,128)S(1)}, f32[1,128]{1,0:T(1,128)S(1)}, u32[]{:S(2)}, u32[]{:S(2)}) collective-permute-start(f32[1,128]{1,0:T(1,128)S(1)} %add_add_fusion.4), channel_id=1, source_target_pairs={{0,3},{1,2},{2,1},{3,0},{4,7},{5,6},{6,5},{7,4},{8,11},{9,10},{10,... | collective-permute-start | bytes 1544 | tf_op jit(solution)/shard_map/ppermute | solution.py:48
  189.9 48.2 %collective-permute-start.56 = (f32[128,1024]{1,0:T(8,128)S(1)}, f32[128,1024]{1,0:T(8,128)S(1)}, u32[]{:S(2)}, u32[]{:S(2)}) collective-permute-start(f32[128,1024]{1,0:T(8,128)S(1)} %copy-done.13), channel_id=1, source_target_pairs={{0,8},{4,12},{8,0},{12,4},{16,24},{20,28},{24,16},{28,20},{1,9},{5... | collective-permute-start | bytes 1572872 | tf_op jit(solution)/shard_map/ppermute | solution.py:48
  190.0 48.8 %collective-permute-start.52 = (f32[128,1024]{1,0:T(8,128)S(1)}, f32[128,1024]{1,0:T(8,128)S(1)}, u32[]{:S(2)}, u32[]{:S(2)}) collective-permute-start(f32[128,1024]{1,0:T(8,128)S(1)} %copy-done.12), channel_id=1, source_target_pairs={{0,8},{4,12},{8,0},{12,4},{16,24},{20,28},{24,16},{28,20},{1,9},{5... | collective-permute-start | bytes 1572872 | tf_op jit(solution)/shard_map/ppermute | solution.py:48
  192.0 31.0 %collective-permute-start.44 = (f32[128,512]{1,0:T(8,128)}, f32[128,512]{1,0:T(8,128)S(1)}, u32[]{:S(2)}, u32[]{:S(2)}) collective-permute-start(f32[128,512]{1,0:T(8,128)} %get-tuple-element.54), channel_id=1, source_target_pairs={{0,8},{4,12},{8,0},{12,4},{16,24},{20,28},{24,16},{28,20},{1,9},{5... | collective-permute-start | bytes 786440 | tf_op jit(solution)/shard_map/ppermute | solution.py:48
  192.9 46.1 %collective-permute-start.40 = (f32[128,1024]{1,0:T(8,128)S(1)}, f32[128,1024]{1,0:T(8,128)S(1)}, u32[]{:S(2)}, u32[]{:S(2)}) collective-permute-start(f32[128,1024]{1,0:T(8,128)S(1)} %copy-done.11), channel_id=1, source_target_pairs={{0,8},{4,12},{8,0},{12,4},{16,24},{20,28},{24,16},{28,20},{1,9},{5... | collective-permute-start | bytes 1572872 | tf_op jit(solution)/shard_map/ppermute | solution.py:48
  194.1 60.2 %collective-permute-start.36 = (f32[4,10,32,256]{3,2,1,0:T(8,128)}, f32[4,10,32,256]{3,2,1,0:T(8,128)S(1)}, u32[]{:S(2)}, u32[]{:S(2)}) collective-permute-start(f32[4,10,32,256]{3,2,1,0:T(8,128)} %get-tuple-element.50), channel_id=1, source_target_pairs={{0,4},{4,0},{8,12},{12,8},{16,20},{20,16},{24,28},{28,24},{1,5},{5... | collective-permute-start | bytes 3932168 | tf_op jit(solution)/shard_map/ppermute | solution.py:48
  194.3 44.7 %copy-start.5 = (f32[128,1024]{1,0:T(8,128)S(1)}, f32[128,1024]{1,0:T(8,128)}, u32[]{:S(2)}) copy-start(f32[128,1024]{1,0:T(8,128)} %get-tuple-element.57) | copy-start | bytes 1572868
  223.1 7.4 %collective-permute-start.50 = (f32[64,512]{1,0:T(8,128)S(1)}, f32[64,512]{1,0:T(8,128)S(1)}, u32[]{:S(2)}, u32[]{:S(2)}) collective-permute-start(f32[64,512]{1,0:T(8,128)S(1)} %slice_add_fusion.10), channel_id=1, source_target_pairs={{0,16},{4,20},{8,24},{12,28},{16,0},{20,4},{24,8},{28,12},{1,17},{... | collective-permute-start | bytes 393224 | tf_op jit(solution)/shard_map/ppermute | solution.py:48
  230.4 7.7 %collective-permute-start.46 = (f32[64,512]{1,0:T(8,128)S(1)}, f32[64,512]{1,0:T(8,128)S(1)}, u32[]{:S(2)}, u32[]{:S(2)}) collective-permute-start(f32[64,512]{1,0:T(8,128)S(1)} %slice_add_fusion.11), channel_id=1, source_target_pairs={{0,16},{4,20},{8,24},{12,28},{16,0},{20,4},{24,8},{28,12},{1,17},{... | collective-permute-start | bytes 393224 | tf_op jit(solution)/shard_map/ppermute | solution.py:48
  238.2 19.5 %collective-permute-start.33 = (f32[4,10,32,256]{3,2,1,0:T(8,128)S(1)}, f32[4,10,32,256]{3,2,1,0:T(8,128)S(1)}, u32[]{:S(2)}, u32[]{:S(2)}) collective-permute-start(f32[4,10,32,256]{3,2,1,0:T(8,128)S(1)} %copy-done.10), channel_id=1, source_target_pairs={{0,4},{4,0},{8,12},{12,8},{16,20},{20,16},{24,28},{28,24},{1,5},{5... | collective-permute-start | bytes 3932168 | tf_op jit(solution)/shard_map/ppermute | solution.py:48
  238.2 41.8 %collective-permute-start.49 = (f32[32,512]{1,0:T(8,128)S(1)}, f32[32,512]{1,0:T(8,128)S(1)}, u32[]{:S(2)}, u32[]{:S(2)}) collective-permute-start(f32[32,512]{1,0:T(8,128)S(1)} %get-tuple-element.69), channel_id=1, source_target_pairs={{0,4},{4,0},{8,12},{12,8},{16,20},{20,16},{24,28},{28,24},{1,5},{5... | collective-permute-start | bytes 196616 | tf_op jit(solution)/shard_map/ppermute | solution.py:48
  238.8 41.7 %collective-permute-start.51 = (f32[32,512]{1,0:T(8,128)S(1)}, f32[32,512]{1,0:T(8,128)S(1)}, u32[]{:S(2)}, u32[]{:S(2)}) collective-permute-start(f32[32,512]{1,0:T(8,128)S(1)} %get-tuple-element.79), channel_id=1, source_target_pairs={{0,4},{4,0},{8,12},{12,8},{16,20},{20,16},{24,28},{28,24},{1,5},{5... | collective-permute-start | bytes 196616 | tf_op jit(solution)/shard_map/ppermute | solution.py:48
  239.0 15.3 %collective-permute-start.58 = (f32[64,1024]{1,0:T(8,128)S(1)}, f32[64,1024]{1,0:T(8,128)S(1)}, u32[]{:S(2)}, u32[]{:S(2)}) collective-permute-start(f32[64,1024]{1,0:T(8,128)S(1)} %slice_add_fusion.3), channel_id=1, source_target_pairs={{0,16},{4,20},{8,24},{12,28},{16,0},{20,4},{24,8},{28,12},{1,17},{... | collective-permute-start | bytes 786440 | tf_op jit(solution)/shard_map/ppermute | solution.py:48
  254.3 20.4 %collective-permute-start.54 = (f32[64,1024]{1,0:T(8,128)S(1)}, f32[64,1024]{1,0:T(8,128)S(1)}, u32[]{:S(2)}, u32[]{:S(2)}) collective-permute-start(f32[64,1024]{1,0:T(8,128)S(1)} %slice_add_fusion.4), channel_id=1, source_target_pairs={{0,16},{4,20},{8,24},{12,28},{16,0},{20,4},{24,8},{28,12},{1,17},{... | collective-permute-start | bytes 786440 | tf_op jit(solution)/shard_map/ppermute | solution.py:48
  254.4 25.6 %collective-permute-start.42 = (f32[64,1024]{1,0:T(8,128)S(1)}, f32[64,1024]{1,0:T(8,128)S(1)}, u32[]{:S(2)}, u32[]{:S(2)}) collective-permute-start(f32[64,1024]{1,0:T(8,128)S(1)} %slice_add_fusion.5), channel_id=1, source_target_pairs={{0,16},{4,20},{8,24},{12,28},{16,0},{20,4},{24,8},{28,12},{1,17},{... | collective-permute-start | bytes 786440 | tf_op jit(solution)/shard_map/ppermute | solution.py:48
  257.7 22.9 %collective-permute-start.37 = (f32[2,1,10,32,256]{4,3,2,1,0:T(8,128)S(1)}, f32[2,1,10,32,256]{4,3,2,1,0:T(8,128)S(1)}, u32[]{:S(2)}, u32[]{:S(2)}) collective-permute-start(f32[2,1,10,32,256]{4,3,2,1,0:T(8,128)S(1)} %slice.209), channel_id=1, source_target_pairs={{0,1},{1,0},{2,3},{3,2},{4,5},{5,4},{6,7},{7,6},{8,9},{9,8},{10,11... | collective-permute-start | bytes 1966088 | tf_op jit(solution)/shard_map/ppermute | solution.py:48
  274.7 17.6 %collective-permute-start.34 = (f32[1,2,10,32,256]{4,3,2,1,0:T(8,128)S(1)}, f32[1,2,10,32,256]{4,3,2,1,0:T(8,128)S(1)}, u32[]{:S(2)}, u32[]{:S(2)}) collective-permute-start(f32[1,2,10,32,256]{4,3,2,1,0:T(8,128)S(1)} %slice_bitcast_fusion), channel_id=1, source_target_pairs={{0,2},{1,3},{2,0},{3,1},{4,6},{5,7},{6,4},{7,5},{8,10},{9,11},{10,... | collective-permute-start | bytes 1966088 | tf_op jit(solution)/shard_map/ppermute | solution.py:48
  279.9 1.3 collective-permute-start.57
  279.9 1.6 collective-permute-start.53
  280.5 1.3 collective-permute-start.59
  280.6 1.4 collective-permute-start.55
  281.3 17.0 %collective-permute-start.45 = (f32[32,512]{1,0:T(8,128)S(1)}, f32[32,512]{1,0:T(8,128)S(1)}, u32[]{:S(2)}, u32[]{:S(2)}) collective-permute-start(f32[32,512]{1,0:T(8,128)S(1)} %get-tuple-element.71), channel_id=1, source_target_pairs={{0,4},{4,0},{8,12},{12,8},{16,20},{20,16},{24,28},{28,24},{1,5},{5... | collective-permute-start | bytes 196616 | tf_op jit(solution)/shard_map/ppermute | solution.py:48
  281.5 16.8 %collective-permute-start.47 = (f32[32,512]{1,0:T(8,128)S(1)}, f32[32,512]{1,0:T(8,128)S(1)}, u32[]{:S(2)}, u32[]{:S(2)}) collective-permute-start(f32[32,512]{1,0:T(8,128)S(1)} %get-tuple-element.81), channel_id=1, source_target_pairs={{0,4},{4,0},{8,12},{12,8},{16,20},{20,16},{24,28},{28,24},{1,5},{5... | collective-permute-start | bytes 196616 | tf_op jit(solution)/shard_map/ppermute | solution.py:48
  281.9 16.5 %collective-permute-start.41 = (f32[32,1024]{1,0:T(8,128)S(1)}, f32[32,1024]{1,0:T(8,128)S(1)}, u32[]{:S(2)}, u32[]{:S(2)}) collective-permute-start(f32[32,1024]{1,0:T(8,128)S(1)} %get-tuple-element.67), channel_id=1, source_target_pairs={{0,4},{4,0},{8,12},{12,8},{16,20},{20,16},{24,28},{28,24},{1,5},{5... | collective-permute-start | bytes 393224 | tf_op jit(solution)/shard_map/ppermute | solution.py:48
  282.1 15.6 %collective-permute-start.38 = (f32[1,1,10,32,256]{4,3,2,1,0:T(8,128)S(1)}, f32[1,1,10,32,256]{4,3,2,1,0:T(8,128)S(1)}, u32[]{:S(2)}, u32[]{:S(2)}) collective-permute-start(f32[1,1,10,32,256]{4,3,2,1,0:T(8,128)S(1)} %slice.211), channel_id=1, source_target_pairs={{0,2},{1,3},{2,0},{3,1},{4,6},{5,7},{6,4},{7,5},{8,10},{9,11},{10,... | collective-permute-start | bytes 983048 | tf_op jit(solution)/shard_map/ppermute | solution.py:48
  292.3 6.0 %collective-permute-start.43 = (f32[32,1024]{1,0:T(8,128)S(1)}, f32[32,1024]{1,0:T(8,128)S(1)}, u32[]{:S(2)}, u32[]{:S(2)}) collective-permute-start(f32[32,1024]{1,0:T(8,128)S(1)} %get-tuple-element.77), channel_id=1, source_target_pairs={{0,4},{4,0},{8,12},{12,8},{16,20},{20,16},{24,28},{28,24},{1,5},{5... | collective-permute-start | bytes 393224 | tf_op jit(solution)/shard_map/ppermute | solution.py:48
  297.7 8.1 %collective-permute-start.35 = (f32[1,1,10,32,256]{4,3,2,1,0:T(8,128)S(1)}, f32[1,1,10,32,256]{4,3,2,1,0:T(8,128)S(1)}, u32[]{:S(2)}, u32[]{:S(2)}) collective-permute-start(f32[1,1,10,32,256]{4,3,2,1,0:T(8,128)S(1)} %slice.207), channel_id=1, source_target_pairs={{0,1},{1,0},{2,3},{3,2},{4,5},{5,4},{6,7},{7,6},{8,9},{9,8},{10,11... | collective-permute-start | bytes 983048 | tf_op jit(solution)/shard_map/ppermute | solution.py:48
  298.2 15.3 %collective-permute-start.39 = (f32[10,32,256]{2,1,0:T(8,128)S(1)}, f32[10,32,256]{2,1,0:T(8,128)S(1)}, u32[]{:S(2)}, u32[]{:S(2)}) collective-permute-start(f32[10,32,256]{2,1,0:T(8,128)S(1)} %fusion.1), channel_id=1, source_target_pairs={{0,16},{4,20},{8,24},{12,28},{16,0},{20,4},{24,8},{28,12},{1,17},{... | collective-permute-start | bytes 983048 | tf_op jit(solution)/shard_map/ppermute | solution.py:48
  (13 other events, 153.9 us)
